TPU v7x, 32 devices: a whole 2x2x4 slice. The times are simulated.
32 devices in a mesh: dp: 8 (over z, y), tensor: 4 (over x, core).
Axes of the slice: x: 2, y: 2, z: 4, core: 2. Of those that a mesh axis runs over, the one named last changes fastest.
Arguments:
- tokens: bfloat16 [8192, 1536], P('dp', 'tensor'), may hold values from -6 to 6
- segments: int32 [8, 1024], P('dp'), may hold values from 0 to 7, never falling along the last dimension, each value on 1 to 512 neighbouring positions
- attn_gain: bfloat16 [1536], P('tensor'), may hold values from 0.25 to 1.75
- w_qkv: bfloat16 [3, 1536, 1536], P(None, None, 'tensor'), may hold values from -0.15625 to 0.15625
- kq_kernel: float32 [16, 6, 11], P('tensor'), may hold values from -0.8 to 1.8
- head_mix: float32 [16, 2], P('tensor'), may hold values from -0.6 to 1.3
- group_gain: bfloat16 [1536], P('tensor'), may hold values from 0.25 to 1.75
- w_out: bfloat16 [1536, 1536], P('tensor'), may hold values from -0.15625 to 0.15625
- mlp_gain: bfloat16 [1536], P('tensor'), may hold values from 0.25 to 1.75
- w_gate_up: bfloat16 [2, 1536, 4096], P(None, None, 'tensor'), may hold values from -0.15625 to 0.15625
- w_down: bfloat16 [4096, 1536], P('tensor'), may hold values from -0.09375 to 0.09375
- cotangent: bfloat16 [8192, 1536], P('dp', 'tensor'), may hold values from -6 to 6
Outputs:
- layer_out: bfloat16 [8192, 1536], P('dp', 'tensor')
- tokens_grad: float32 [8192, 1536], P('dp', 'tensor')
- attn_gain_grad: float32 [1536], P('tensor')
- w_qkv_grad: float32 [3, 1536, 1536], P(None, None, 'tensor')
- kq_kernel_grad: float32 [16, 6, 11], P('tensor')
- head_mix_grad: float32 [16, 2], P('tensor')
- group_gain_grad: float32 [1536], P('tensor')
- w_out_grad: float32 [1536, 1536], P('tensor')
- mlp_gain_grad: float32 [1536], P('tensor')
- w_gate_up_grad: float32 [2, 1536, 4096], P(None, None, 'tensor')
- w_down_grad: float32 [4096, 1536], P('tensor')
Inputs may be any that keep to these rules, and one draw needn't show every extreme that they name: `segments`: within a sequence the numbers never fall; each document holds at most 512 tokens.
All inputs are finite; a program needn't handle non-finite values.
Results may differ from a plain program's by a relative error of at most 0.018.
The roundings to bfloat16 on the way count: a program that leaves them out, or rounds other values in their place, can miss the bound.
Values may be sent and summed in bfloat16 or wider, within the bound.
A program may use at most 320 MiB of HBM per device.

v0:
```python
import jax
import jax.numpy as jnp
from jax import lax
from jax.sharding import PartitionSpec as P

HEAD_DIM = 96


EPS = 1e-05
NEG = -1e30
HIGH = lax.Precision.HIGHEST


def valid_pairs(seg_row):
    length = seg_row.shape[0]
    place = lax.iota(jnp.int32, length)
    return (place[None, :] <= place[:, None]) & (seg_row[:, None] == seg_row[None, :])


def padded_scores(masked, kernel):
    query_taps = kernel.shape[1]
    key_half = kernel.shape[2] // 2
    return jnp.pad(masked, ((0, 0), (query_taps - 1, 0), (key_half, key_half)))


def conv_window(padded, kernel, query_shift, key_shift, length):
    query_taps = kernel.shape[1]
    key_taps = kernel.shape[2]
    row_start = query_taps - 1 - query_shift
    col_start = key_taps - 1 - key_shift
    return lax.slice(
        padded, (0, row_start, col_start), (padded.shape[0], row_start + length, col_start + length)
    )


def kq_conv(masked, kernel):
    length = masked.shape[1]
    padded = padded_scores(masked, kernel)
    summed = jnp.zeros(masked.shape, jnp.float32)
    for query_shift in range(kernel.shape[1]):
        for key_shift in range(kernel.shape[2]):
            shifted = conv_window(padded, kernel, query_shift, key_shift, length)
            summed = summed + kernel[:, query_shift, key_shift][:, None, None] * shifted
    return summed


def conv_back(grad_logits, masked, kernel):
    query_taps = kernel.shape[1]
    key_taps = kernel.shape[2]
    key_half = key_taps // 2
    heads_here = masked.shape[0]
    length = masked.shape[1]
    padded_in = padded_scores(masked, kernel)
    padded_grad = jnp.pad(grad_logits, ((0, 0), (0, query_taps - 1), (key_half, key_half)))
    grad_masked = jnp.zeros(masked.shape, jnp.float32)
    kernel_terms = []
    for query_shift in range(query_taps):
        for key_shift in range(key_taps):
            window_in = conv_window(padded_in, kernel, query_shift, key_shift, length)
            window_grad = lax.slice(
                padded_grad,
                (0, query_shift, key_shift),
                (heads_here, query_shift + length, key_shift + length),
            )
            grad_masked = (
                grad_masked + kernel[:, query_shift, key_shift][:, None, None] * window_grad
            )
            kernel_terms.append(jnp.sum(grad_logits * window_in, axis=(1, 2)))
    grad_kernel = jnp.stack(kernel_terms, axis=1).reshape(heads_here, query_taps, key_taps)
    return (grad_masked, grad_kernel)


def mix_heads(probs, mix):
    heads_here = probs.shape[0]
    length = probs.shape[1]
    paired = probs.reshape(heads_here // 2, 2, length, length)
    weights = mix.reshape(heads_here // 2, 2, 2)
    first = weights[:, :, 0][:, :, None, None] * paired[:, 0][:, None]
    second = weights[:, :, 1][:, :, None, None] * paired[:, 1][:, None]
    return (first + second).reshape(heads_here, length, length)


def mix_back(grad_mixed, probs, mix):
    heads_here = probs.shape[0]
    length = probs.shape[1]
    paired_grad = grad_mixed.reshape(heads_here // 2, 2, length, length)
    paired = probs.reshape(heads_here // 2, 2, length, length)
    weights = mix.reshape(heads_here // 2, 2, 2)
    grad_probs = (
        weights[:, 0, :][:, :, None, None] * paired_grad[:, 0][:, None]
        + weights[:, 1, :][:, :, None, None] * paired_grad[:, 1][:, None]
    )
    grad_mix = jnp.einsum("grqk,gsqk->grs", paired_grad, paired, precision=HIGH)
    return (grad_probs.reshape(heads_here, length, length), grad_mix.reshape(heads_here, 2))


def score_logits(query, keys, seg_row, kernel):
    scale = query.shape[2] ** (-0.5)
    valid = valid_pairs(seg_row)[None]
    raw = jnp.einsum("qhd,khd->hqk", query, keys, preferred_element_type=jnp.float32)
    masked = jnp.where(valid, raw * scale, 0.0)
    logits = jnp.where(valid, kq_conv(masked, kernel), NEG)
    return (valid, masked, logits)


def attend_forward(query, keys, values, seg_row, kernel, mix):
    valid, masked, logits = score_logits(query, keys, seg_row, kernel)
    peak = jnp.max(logits, axis=-1, keepdims=True)
    expo = jnp.exp(logits - peak)
    summed = jnp.sum(expo, axis=-1, keepdims=True)
    probs = expo / summed
    mixed = mix_heads(probs, mix).astype(jnp.bfloat16)
    output = jnp.einsum("hqk,khd->qhd", mixed, values, preferred_element_type=jnp.float32)
    return (output, (peak + jnp.log(summed))[..., 0])


def attend_backward(query, keys, values, seg_row, grad_out, log_norm, kernel, mix):
    scale = query.shape[2] ** (-0.5)
    valid, masked, logits = score_logits(query, keys, seg_row, kernel)
    probs = jnp.exp(logits - log_norm[..., None])
    mixed = mix_heads(probs, mix).astype(jnp.bfloat16)
    grad_values = jnp.einsum("hqk,qhd->khd", mixed, grad_out, preferred_element_type=jnp.float32)
    grad_mixed = jnp.einsum("qhd,khd->hqk", grad_out, values, preferred_element_type=jnp.float32)
    grad_probs, grad_mix = mix_back(grad_mixed, probs, mix)
    grad_logits = probs * (grad_probs - jnp.sum(grad_probs * probs, axis=-1, keepdims=True))
    grad_masked, grad_kernel = conv_back(grad_logits, masked, kernel)
    grad_scores = (jnp.where(valid, grad_masked, 0.0) * scale).astype(jnp.bfloat16)
    grad_query = jnp.einsum("hqk,khd->qhd", grad_scores, keys, preferred_element_type=jnp.float32)
    grad_keys = jnp.einsum("hqk,qhd->khd", grad_scores, query, preferred_element_type=jnp.float32)
    return (grad_query, grad_keys, grad_values, grad_kernel, grad_mix)


def contract_rows(left, right):
    return lax.dot_general(
        left, right, (((0,), (0,)), ((), ())), preferred_element_type=jnp.float32
    )


def contract_cols(left, right):
    return lax.dot_general(
        left, right, (((1,), (1,)), ((), ())), preferred_element_type=jnp.float32
    )


def on_device(
    tokens,
    segments,
    attn_gain,
    w_qkv,
    kq_kernel,
    head_mix,
    group_gain,
    w_out,
    mlp_gain,
    w_gate_up,
    w_down,
    cotangent,
):
    rank = lax.axis_index("tensor")
    rows_here = tokens.shape[0]
    local_width = tokens.shape[1]
    seq_count = segments.shape[0]
    length = segments.shape[1]
    heads_here = w_qkv.shape[2] // HEAD_DIM
    start = rank * local_width
    gathered, gain_one, gain_two = (
        lax.all_gather(tokens, "tensor", axis=1, tiled=True),
        lax.all_gather(attn_gain, "tensor", axis=0, tiled=True),
        lax.all_gather(mlp_gain, "tensor", axis=0, tiled=True),
    )
    resid = gathered.astype(jnp.float32)
    full_width = resid.shape[1]
    scale_one = lax.rsqrt(jnp.mean(resid * resid, axis=-1, keepdims=True) + EPS)
    unit_one = resid * scale_one
    normed_one = (unit_one * gain_one.astype(jnp.float32)).astype(jnp.bfloat16)
    projected = jnp.einsum(
        "td,cde->cte", normed_one, w_qkv, preferred_element_type=jnp.float32
    ).astype(jnp.bfloat16)
    split_heads = projected.reshape(3, seq_count, length, heads_here, HEAD_DIM)

    def forward_one(items):
        return attend_forward(items[0], items[1], items[2], items[3], kq_kernel, head_mix)

    heads_out, log_norms = lax.map(
        forward_one, (split_heads[0], split_heads[1], split_heads[2], segments)
    )
    heads_out = heads_out.reshape(rows_here, heads_here, HEAD_DIM)
    group_scale = lax.rsqrt(jnp.mean(heads_out * heads_out, axis=-1, keepdims=True) + EPS)
    unit_heads = heads_out * group_scale
    gain_heads = group_gain.astype(jnp.float32).reshape(heads_here, HEAD_DIM)
    grouped = (unit_heads * gain_heads).astype(jnp.bfloat16).reshape(rows_here, local_width)
    attn_part = jnp.dot(grouped, w_out, preferred_element_type=jnp.float32)
    gain_full = gain_two.astype(jnp.float32)
    attn = lax.psum(attn_part, "tensor")
    hidden = resid + attn
    scale_two = lax.rsqrt(jnp.mean(hidden * hidden, axis=-1, keepdims=True) + EPS)
    unit_two = hidden * scale_two
    normed_two = (unit_two * gain_full).astype(jnp.bfloat16)
    hidden_local = lax.dynamic_slice_in_dim(hidden, start, local_width, 1)
    gate_up = jnp.einsum("td,cdf->ctf", normed_two, w_gate_up, preferred_element_type=jnp.float32)
    gate = gate_up[0]
    up = gate_up[1]
    sigmoid = jax.nn.sigmoid(gate)
    swish = gate * sigmoid
    act = (swish * up).astype(jnp.bfloat16)
    mlp_part = jnp.dot(act, w_down, preferred_element_type=jnp.float32)
    mlp_local = lax.psum_scatter(
        mlp_part.astype(jnp.bfloat16), "tensor", scatter_dimension=1, tiled=True
    ).astype(jnp.float32)
    layer_out = (hidden_local + mlp_local).astype(jnp.bfloat16)
    full_cot = lax.all_gather(cotangent, "tensor", axis=1, tiled=True)
    grad_down = contract_rows(act, full_cot)
    grad_act = contract_cols(full_cot, w_down)
    grad_gate = grad_act * up * sigmoid * (1.0 + gate * (1.0 - sigmoid))
    grad_up = grad_act * swish
    grad_pair = jnp.stack([grad_gate, grad_up]).astype(jnp.bfloat16)
    grad_gate_up = jnp.einsum(
        "td,ctf->cdf", normed_two, grad_pair, preferred_element_type=jnp.float32
    )
    grad_two_part = jnp.einsum(
        "ctf,cdf->td", grad_pair, w_gate_up, preferred_element_type=jnp.float32
    )
    grad_two = lax.psum(grad_two_part, "tensor")
    grad_gain_two = lax.dynamic_slice_in_dim(
        jnp.sum(grad_two * unit_two, axis=0), start, local_width, 0
    )
    scaled_two = grad_two * gain_full
    grad_hidden = full_cot.astype(jnp.float32) + scale_two * (
        scaled_two - unit_two * jnp.mean(scaled_two * unit_two, axis=-1, keepdims=True)
    )
    grad_attn = grad_hidden.astype(jnp.bfloat16)
    grad_hidden_local = lax.dynamic_slice_in_dim(grad_hidden, start, local_width, 1)
    grad_w_out = contract_rows(grouped, grad_attn)
    grad_grouped = contract_cols(grad_attn, w_out).reshape(rows_here, heads_here, HEAD_DIM)
    grad_group_gain = jnp.sum(grad_grouped * unit_heads, axis=0).reshape(local_width)
    scaled_heads = grad_grouped * gain_heads
    grad_heads = (
        group_scale
        * (scaled_heads - unit_heads * jnp.mean(scaled_heads * unit_heads, axis=-1, keepdims=True))
    ).astype(jnp.bfloat16)
    grad_split = grad_heads.reshape(seq_count, length, heads_here, HEAD_DIM)

    def backward_one(items):
        return attend_backward(
            items[0], items[1], items[2], items[3], items[4], items[5], kq_kernel, head_mix
        )

    grad_query, grad_keys, grad_values, kernel_terms, mix_terms = lax.map(
        backward_one,
        (split_heads[0], split_heads[1], split_heads[2], segments, grad_split, log_norms),
    )
    grad_proj = (
        jnp.stack([grad_query, grad_keys, grad_values])
        .astype(jnp.bfloat16)
        .reshape(3, rows_here, local_width)
    )
    grad_kernel = jnp.sum(kernel_terms, axis=0)
    grad_mix = jnp.sum(mix_terms, axis=0)
    grad_qkv = jnp.einsum("td,cte->cde", normed_one, grad_proj, preferred_element_type=jnp.float32)
    grad_one_part = jnp.einsum("cte,cde->td", grad_proj, w_qkv, preferred_element_type=jnp.float32)
    grad_one = lax.psum_scatter(
        grad_one_part.astype(jnp.bfloat16), "tensor", scatter_dimension=1, tiled=True
    ).astype(jnp.float32)
    unit_local = lax.dynamic_slice_in_dim(unit_one, start, local_width, 1)
    scaled_one = grad_one * attn_gain.astype(jnp.float32)
    row_total = lax.psum(jnp.sum(scaled_one * unit_local, axis=-1, keepdims=True), "tensor")
    tokens_grad = grad_hidden_local + scale_one * (
        scaled_one - unit_local * (row_total / full_width)
    )
    grad_gain_one = jnp.sum(grad_one * unit_local, axis=0)
    (
        grad_gain_one,
        grad_qkv,
        grad_kernel,
        grad_mix,
        grad_group_gain,
        grad_w_out,
        grad_gain_two,
        grad_gate_up,
        grad_down,
    ) = lax.psum(
        (
            grad_gain_one,
            grad_qkv,
            grad_kernel,
            grad_mix,
            grad_group_gain,
            grad_w_out,
            grad_gain_two,
            grad_gate_up,
            grad_down,
        ),
        "dp",
    )
    return (
        layer_out,
        tokens_grad,
        grad_gain_one,
        grad_qkv,
        grad_kernel,
        grad_mix,
        grad_group_gain,
        grad_w_out,
        grad_gain_two,
        grad_gate_up,
        grad_down,
    )


def solution(mesh):
    in_specs = (
        P("dp", "tensor"),
        P("dp", None),
        P("tensor"),
        P(None, None, "tensor"),
        P("tensor", None, None),
        P("tensor", None),
        P("tensor"),
        P("tensor", None),
        P("tensor"),
        P(None, None, "tensor"),
        P("tensor", None),
        P("dp", "tensor"),
    )
    out_specs = (
        P("dp", "tensor"),
        P("dp", "tensor"),
        P("tensor"),
        P(None, None, "tensor"),
        P("tensor", None, None),
        P("tensor", None),
        P("tensor"),
        P("tensor", None),
        P("tensor"),
        P(None, None, "tensor"),
        P("tensor", None),
    )
    return jax.shard_map(
        on_device, mesh=mesh, in_specs=in_specs, out_specs=out_specs, check_vma=False
    )
```

profile of v0, /device:TPU:0, one launch (start us, length us, event | category | flops | bytes accessed | tf_op | source)
XLA Modules:
  0.0 3078.3 jit_solution(3075463424177838024)
XLA Ops:
  12.3 6.1 all-gather
  29.7 11.2 all-gather.5.cloned.1.call-done
  43.5 6.0 convert_bitcast_fusion
  50.7 8.6 multiply_select_fusion
  59.3 754.6 %fusion.168 = (f32[4,1024]{1,0:T(4,128)S(1)}, f32[4,1024,1024]{2,1,0:T(8,128)}) fusion(f32[4]{0:T(128)} %get-tuple-element.249, f32[4]{0:T(128)} %get-tuple-element.250, f32[4]{0:T(128)} %get-tuple-element.186, f32[4]{0:T(128)} %get-tuple-element.187, f32[4]{0:T(128)} %get-tuple-element.188, f32[4]{0:T(128)} %get-tuple-element.189, ...), kind=kLoop, calls=%fused_computation.489 | loop fusion | flops 557838336 | bytes 34620448 | tf_op jit(solution)/shard_map/while/body/eval_jaxpr/reduce_max | solution.py:108
  813.9 7.8 fusion.140
  824.5 4.7 fusion.139
  829.3 7.6 slice_bitcast_fusion.5
  836.9 7.4 fusion.138
  849.3 4.6 fusion.172
  855.3 5.1 all-gather.1
  862.4 111.2 %all-reduce.8.cloned.1.call-done = f32[1024,1536]{1,0:T(8,128)} async-done(((f32[1024,1536]{1,0:T(8,128)}), f32[1024,1536]{1,0:T(8,128)}) %all-reduce.8.cloned.1.call-update) | async-done | bytes 6291472 | tf_op jit(solution)/shard_map/psum | solution.py:194
  973.6 7.6 multiply_reduce_fusion.68
  984.2 11.3 convolution_bitcast_fusion.3
  995.5 8.4 all-gather.7.cloned.1.call-done
  1003.9 11.5 fusion.147
  1017.4 10.5 convolution_bitcast_fusion.2
  1035.9 7.6 convolution_convert_fusion
  1043.5 4.7 copy.137
  1048.3 99.3 %all-reduce.10.cloned.1.call-done = f32[1024,1536]{1,0:T(8,128)} async-done(((f32[1024,1536]{1,0:T(8,128)}), f32[1024,1536]{1,0:T(8,128)}) %all-reduce.10.cloned.1.call-update) | async-done | bytes 6291472 | tf_op jit(solution)/shard_map/psum | solution.py:223
  1147.6 6.4 multiply_reduce_fusion.66
  1154.0 5.9 multiply_add_fusion
  1166.3 7.1 slice_bitcast_fusion.3
  1173.4 4.1 copy-done.2
  1177.5 21.4 fusion.134
  1199.0 101.0 %multiply_reduce_fusion.54 = (f32[4]{0:T(128)}, f32[4]{0:T(128)}, f32[4]{0:T(128)}, f32[4]{0:T(128)}, f32[4]{0:T(128)}, /*index=5*/f32[4]{0:T(128)}, f32[4]{0:T(...) fusion(f32[4,1024,1024]{2,1,0:T(8,128)} %multiply_select_fusion, ...), kind=kOutput, calls=%fused_computation.329 | output fusion | flops 121639920 | bytes 83886304 | tf_op jit(solution)/shard_map/while/body/eval_jaxpr/sub | solution.py:125
  1300.0 771.0 %multiply_convert_fusion = bf16[4,1024,1024]{2,1,0:T(8,128)(2,1)} fusion(f32[4,1024,1024]{2,1,0:T(8,128)} %get-tuple-element.285, f32[4]{0:T(128)} %get-tuple-element.249, f32[4]{0:T(128)} %get-tuple-element.250, f32[4]{0:T(128)} %get-tuple-element.186, f32[4]{0:T(128)} %get-tuple-element.187, f32[4]{0:T(128)} %get-tuple-element.188, ...), kind=kLoop, calls=%fused_computation.341 | loop fusion | flops 562036736 | bytes 26215456 | tf_op jit(solution)/shard_map/while/body/eval_jaxpr/convert_element_type | solution.py:127
  2071.0 7.2 convolution_convert_fusion.3
  2080.5 6.0 convolution_convert_fusion.2
  2088.8 6.7 slice_bitcast_fusion.1
  2103.1 7.3 bitcast_convert_fusion
  2110.3 4.6 copy.139
  2115.1 9.1 fusion.175
  2124.2 13.9 convolution_bitcast_fusion
  2141.0 6.3 convolution_bitcast_fusion.1
  2148.6 25.6 copy.125
  2174.2 25.6 copy.126
  2211.7 181.0 %multiply_reduce_fusion.36 = (f32[4]{0:T(128)}, f32[4]{0:T(128)}, f32[4]{0:T(128)}, f32[4]{0:T(128)}, f32[4]{0:T(128)}, /*index=5*/f32[4]{0:T(128)}, f32[4]{0:T(...) fusion(f32[4,1024,1024]{2,1,0:T(8,128)} %get-tuple-element.285,, ...), kind=kLoop, calls=%fused_computation.311 | loop fusion | flops 150994912 | bytes 33554720 | tf_op jit(solution)/shard_map/while/body/eval_jaxpr/reduce_sum | solution.py:68
  2415.5 186.3 %multiply_reduce_fusion.18 = (f32[4]{0:T(128)}, f32[4]{0:T(128)}, f32[4]{0:T(128)}, f32[4]{0:T(128)}, f32[4]{0:T(128)}, /*index=5*/f32[4]{0:T(128)}, f32[4]{0:T(...) fusion(f32[4,1024,1024]{2,1,0:T(8,128)} %get-tuple-element.285,, ...), kind=kLoop, calls=%fused_computation.293 | loop fusion | flops 150994912 | bytes 33554720 | tf_op jit(solution)/shard_map/while/body/eval_jaxpr/reduce_sum | solution.py:68
  2604.4 174.2 %multiply_reduce_fusion = (f32[4]{0:T(128)}, f32[4]{0:T(128)}, f32[4]{0:T(128)}, f32[4]{0:T(128)}, f32[4]{0:T(128)}, /*index=5*/f32[4]{0:T(128)}, f32[4]{0:T(128...) fusion(f32[4,1024,1024]{2,1,0:T(8,128)} %get-tuple-element.285,, ...), kind=kLoop, calls=%fused_computation.275 | loop fusion | flops 150994912 | bytes 33554720 | tf_op jit(solution)/shard_map/while/body/eval_jaxpr/reduce_sum | solution.py:68
  2825.1 154.8 %fusion.174 = f32[2,2,2,1]{2,1,3,0:T(2,128)} fusion(f32[2,2,1024,1024]{2,1,3,0:T(2,128)} %copy.125, f32[2,2,1024,1024]{2,1,3,0:T(2,128)} %copy.126), kind=kOutput, calls=%fused_computation.495 | convolution fusion | flops 100663296 | bytes 33554464 | tf_op jit(solution)/shard_map/while/body/eval_jaxpr/grqk,gsqk->grs/dot_general | solution.py:93
  2992.5 38.2 %all-reduce.2 = (f32[384]{0:T(512)}, f32[4,6,11]{2,1,0:T(8,128)}, f32[4,2]{0,1:T(2,128)}, f32[384]{0:T(512)}, f32[384]{0:T(512)}) all-reduce(f32[384]{0:T(512)} %get-tuple-element.181, f32[4,6,11]{2,1,0:T(8,128)S(1)} %reduce_sum.848, f32[4,2]{0,1:T(2,128)} %copy.136, f32[384]{0:T(512)} %reshape.232, ...), channel_id=1, replica_groups=mesh['dp'=8,'tensor'=4] {'dp'}, use_global_device_ids=true, to_apply=%region_15.16 | all-reduce | flops 1424 | bytes 11392 | tf_op jit(solution)/shard_map/psum | solution.py:281
  3031.9 5.8 psum.86
  3037.7 3.6 fusion.152
  3041.4 8.0 copy.129
  3049.4 12.6 copy.131
  3062.0 3.2 copy.147
  3065.3 5.9 copy.148
  (242 shorter events, 164.5 us)
Async XLA Ops:
  7.2 36.3 %copy-start = (bf16[3,1536,384]{2,1,0:T(8,128)(2,1)S(1)}, bf16[3,1536,384]{2,1,0:T(8,128)(2,1)}, u32[]{:S(2)}) copy-start(bf16[3,1536,384]{2,1,0:T(8,128)(2,1)} %param.15) | copy-start | bytes 10616836
  7.2 33.6 %all-gather.5.cloned.1.call-start = ((), (), s32[]{:S(2)}) async-start(), calls=%async_computation.2 | async-start | bytes 3932160 | tf_op jit(solution)/shard_map/all_gather | solution.py:167
  7.9 965.7 %all-reduce.8.cloned.1.call-start = ((), (), s32[]{:S(2)}) async-start(), calls=%async_computation.3 | async-start | bytes 12582912 | tf_op jit(solution)/shard_map/psum | solution.py:194
  11.0 39.6 %copy-start.35 = (f32[2,2,2]{1,0,2:T(2,128)}, f32[2,2,2]{1,0,2:T(2,128)S(1)}, u32[]{:S(2)}) copy-start(f32[2,2,2]{1,0,2:T(2,128)S(1)} %reshape.226) | copy-start | bytes 100
  40.8 9.9 copy-start.5
  43.5 15.8 copy-start.31
  50.7 8.6 copy-start.10
  50.7 8.6 copy-start.11
  813.9 10.6 copy-start.1
  829.3 7.6 copy-start.42
  829.3 7.6 copy-start.44
  836.8 7.5 copy-start.14
  836.8 11.3 copy-start.33
  836.9 12.4 copy-start.18
  853.9 150.0 %all-gather.7.cloned.1.call-start = ((), (), s32[]{:S(2)}) async-start(), calls=%async_computation.4 | async-start | bytes 3932160 | tf_op jit(solution)/shard_map/all_gather | solution.py:211
  854.6 293.0 %all-reduce.10.cloned.1.call-start = ((), (), s32[]{:S(2)}) async-start(), calls=%async_computation.5 | async-start | bytes 12582912 | tf_op jit(solution)/shard_map/psum | solution.py:223
  973.6 10.5 copy-start.26
  1027.9 1954.7 %reduce-scatter.7.cloned.1.call-start = ((), (), s32[]{:S(2)}) async-start(), calls=%async_computation.6 | async-start | bytes 3932160
  1035.9 111.7 %copy-start.27 = (f32[1536]{0:T(1024)S(1)}, f32[1536]{0:T(1024)}, u32[]{:S(2)}) copy-start(f32[1536]{0:T(1024)} %reshape.239) | copy-start | bytes 18436
  1035.9 111.7 %copy-start.30 = (f32[1024]{0:T(1024)S(1)}, f32[1024]{0:T(1024)}, u32[]{:S(2)}) copy-start(f32[1024]{0:T(1024)} %copy-done.29) | copy-start | bytes 12292
  1048.2 1939.4 %reduce-scatter.9.cloned.1.call-start = ((), (), s32[]{:S(2)}) async-start(), calls=%async_computation.7 | async-start | bytes 3932160
  1147.6 6.4 copy-start.6
  1147.6 12.3 copy-start.19
  1154.0 7.4 copy-start.8
  1154.0 7.4 copy-start.24
  1154.0 7.4 copy-start.34
  1154.0 9.9 copy-start.15
  1166.3 11.2 copy-start.2
  1166.3 11.2 copy-start.28
  1166.3 11.2 copy-start.40
  1166.3 11.2 copy-start.41
  1199.0 101.0 %copy-start.38 = (f32[4]{0:T(128)S(1)}, f32[4]{0:T(128)}, u32[]{:S(2)}) copy-start(f32[4]{0:T(128)} %get-tuple-element.204) | copy-start | bytes 52
  2088.8 6.8 copy-start.43
  2088.8 6.8 copy-start.45
  2115.0 926.4 %all-reduce.12.cloned.1.call-start = ((), (), s32[]{:S(2)}) async-start(), calls=%async_computation.8 | async-start | bytes 56623104 | tf_op jit(solution)/shard_map/psum | solution.py:281
  2115.1 23.1 slice-start
  2124.2 14.0 slice-start.1
  2124.2 14.0 copy-start.17
  2124.2 16.8 copy-start.9
  2124.2 16.8 copy-start.20
  2124.2 16.8 copy-start.21
  2124.2 16.8 copy-start.22
  2124.2 16.8 copy-start.32
  2124.2 16.8 copy-start.37
  2174.2 25.6 copy-start.36
  2174.2 26.2 copy-start.48
  2174.2 26.3 copy-start.47
  2174.2 26.4 copy-start.46
  (12 other events, 28.0 us)
Sparse Core Ops, SparseCore 0:
  9.6 31.1 all-gather.4
  854.0 119.5 all-reduce.7
  975.2 28.6 all-gather.6
  1028.0 119.5 all-reduce.9
  1150.0 38.1 reduce-scatter.6
  2115.1 37.7 reduce-scatter.8
  2159.0 836.7 all-reduce.11
where the time goes:
time: 3090 us; the launch traced here: 3080 us
  other arithmetic  2250 us (73%)
  matrix products  276 us (9%)
  local copies, waits for them, and re-layouts  249 us (8%)
  waiting for transfers between devices  232 us (8%)
  blocking collectives  55.1 us (2%)
    convert_element_type x1, other arithmetic, attend_backward(): (jnp.where(valid, grad_masked, 0.0) * scale).astype(jnp.bfloat16)  771 us
    reduce_max x1, other arithmetic, attend_forward(): peak = jnp.max(logits, axis=-1, keepdims=True)  755 us
    reduce_sum x3, other arithmetic, conv_back(): kernel_terms.append(jnp.sum(grad_logits * window_in, axis=(1, 2)))  541 us
    dot_general x1, matrix products, mix_back(): grad_mix = jnp.einsum('grqk,gsqk->grs', paired_grad, paired, precision=HIGH)  155 us
    psum x1, waiting for transfers between devices, on_device(): attn = lax.psum(attn_part, 'tensor')  111 us
    sub x1, other arithmetic, attend_backward(): grad_probs - jnp.sum(grad_probs * probs, axis=-1, keepdims=True)  101 us
    psum x1, waiting for transfers between devices, on_device(): grad_two = lax.psum(grad_two_part, 'tensor')  99.3 us
    another operation x67, local copies, waits for them, and re-layouts, conv_back(): jnp.stack(kernel_terms, axis=1).reshape(heads_here, query_taps, key_taps)  82.4 us
  transfers between devices with their start and end apart: 7, of which 4 were waited for; matrix products, arithmetic and copies ran while one was open for 62% of the time, Pallas kernels for 0%

commit v1 on v0

v1 whole, which is shorter than its diff:
```python
import functools

import jax
import jax.numpy as jnp
from jax import lax
from jax.experimental import pallas as pl
from jax.experimental.pallas import tpu as pltpu
from jax.sharding import PartitionSpec as P

HEAD_DIM = 96
PAD_DIM = 128
DOC_MOST = 512
EPS = 1e-05
NEG = -1e30

ROWS = 128
HALO = 16
WIN = 256
OWN = 16
STEP = WIN - 2 * OWN
TOP = 256
EXT = ROWS + HALO

F32 = jnp.float32
BF16 = jnp.bfloat16


def windows_most(key_half):
    return -(-(DOC_MOST - 1 + ROWS + key_half) // STEP)


def dot_nt(a, b):
    return lax.dot_general(a, b, (((1,), (1,)), ((), ())), preferred_element_type=F32)


def dot_tn(a, b):
    return lax.dot_general(a, b, (((0,), (0,)), ((), ())), preferred_element_type=F32)


def dot_nn(a, b):
    return jnp.dot(a, b, preferred_element_type=F32)


def fill_padded(dst, src, top, length):
    total = dst.shape[0]
    dst[0:top, :] = jnp.zeros((top, dst.shape[1]), dst.dtype)
    dst[top : top + length, :] = src[...]
    if total > top + length:
        dst[top + length : total, :] = jnp.zeros((total - top - length, dst.shape[1]), dst.dtype)


def lanes_between(first, last, width):
    lane = lax.broadcasted_iota(jnp.int32, (first.shape[0], width), 1)
    return (lane >= first) & (lane <= last)


def row_numbers(base, count):
    return base + lax.broadcasted_iota(jnp.int32, (count, 1), 0)


def forward_kernel(
    n_taps, key_half, most, count_ref, mix_ref, q_ref, k_ref, v_ref, start_ref, t_hi_ref, t_lo_ref,
    gain_ref, probs_ref, heads_ref, grouped_ref, qs, ks, vs, logit_ref,
):
    pair = pl.program_id(0)
    block = pl.program_id(1)
    length = q_ref.shape[0]
    scale = HEAD_DIM ** (-0.5)

    @pl.when(block == 0)
    def _():
        fill_padded(qs, q_ref, HALO, length)
        fill_padded(ks, k_ref, TOP, length)
        fill_padded(vs, v_ref, TOP, length)

    row0 = pl.multiple_of(block * ROWS, ROWS)

    def body(n):
        start = start_ref[pl.ds(row0, EXT), :]
        place = row_numbers(row0 - HALO, EXT)
        peaks = [None, None]
        for k in range(n):
            base = row0 + ROWS - STEP * (k + 1) - OWN
            at = pl.multiple_of(TOP + base, 16)
            first = start - base
            last = place - base
            valid = lanes_between(first, last, WIN)
            shown = lanes_between(
                jnp.maximum(first[HALO:], key_half + 1), jnp.minimum(last[HALO:], WIN - 2 - key_half), WIN
            )
            for s in range(2):
                cols = pl.ds(s * PAD_DIM, PAD_DIM)
                raw = dot_nt(qs[pl.ds(row0, EXT), cols], ks[pl.ds(at, WIN), cols])
                masked = jnp.where(valid, raw * scale, 0.0)
                hi = masked.astype(BF16)
                lo = (masked - hi.astype(F32)).astype(BF16)
                total = None
                for a in reversed(range(n_taps)):
                    t_hi = t_hi_ref[s, a]
                    term = dot_nn(hi, t_hi) + dot_nn(lo, t_hi) + dot_nn(hi, t_lo_ref[s, a])
                    total = term if total is None else pltpu.roll(total, 1, 0) + term
                logits = jnp.where(shown, total[HALO:], NEG)
                logit_ref[s, k] = logits
                top = jnp.max(logits, axis=-1, keepdims=True)
                peaks[s] = top if peaks[s] is None else jnp.maximum(peaks[s], top)
        lane = lax.broadcasted_iota(jnp.int32, (ROWS, WIN), 1)
        own = (lane >= OWN) & (lane < WIN - OWN)
        sums = [None, None]
        for k in range(n):
            for s in range(2):
                expo = jnp.exp(logit_ref[s, k] - peaks[s])
                logit_ref[s, k] = expo
                part = jnp.sum(jnp.where(own, expo, 0.0), axis=-1, keepdims=True)
                sums[s] = part if sums[s] is None else sums[s] + part
        inverse = [1.0 / sums[s] for s in range(2)]
        outs = [None, None]
        for k in range(n):
            base = row0 + ROWS - STEP * (k + 1) - OWN
            at = pl.multiple_of(TOP + base, 16)
            probs = []
            for s in range(2):
                prob = logit_ref[s, k] * inverse[s]
                probs_ref[s, 0, k] = prob
                probs.append(jnp.where(own, prob, 0.0))
            for h in range(2):
                mixed = (
                    mix_ref[2 * pair + h, 0] * probs[0] + mix_ref[2 * pair + h, 1] * probs[1]
                ).astype(BF16)
                part = dot_nn(mixed, vs[pl.ds(at, WIN), pl.ds(h * PAD_DIM, PAD_DIM)])
                outs[h] = part if outs[h] is None else outs[h] + part
        for h in range(2):
            cols = slice(h * PAD_DIM, (h + 1) * PAD_DIM)
            out = outs[h]
            heads_ref[:, cols] = out
            factor = lax.rsqrt(jnp.sum(out * out, axis=-1, keepdims=True) * (1.0 / HEAD_DIM) + EPS)
            grouped_ref[:, cols] = (out * factor * gain_ref[:, cols]).astype(BF16)

    for n in range(1, most + 1):
        pl.when(count_ref[block] == n)(functools.partial(body, n))


def attend_forward(proj, start, counts, t_hi, t_lo, mix, gain):
    length = proj.shape[0]
    heads, n_taps = t_hi.shape[:2]
    pairs = heads // 2
    blocks = length // ROWS
    key_half = 5
    most = windows_most(key_half)
    two = 2 * PAD_DIM
    grid_spec = pltpu.PrefetchScalarGridSpec(
        num_scalar_prefetch=2,
        grid=(pairs, blocks),
        in_specs=[
            pl.BlockSpec((length, two), lambda p, b, *_: (0, p)),
            pl.BlockSpec((length, two), lambda p, b, *_: (0, pairs + p)),
            pl.BlockSpec((length, two), lambda p, b, *_: (0, 2 * pairs + p)),
            pl.BlockSpec((HALO + length, 1), lambda p, b, *_: (0, 0)),
            pl.BlockSpec((2, n_taps, WIN, WIN), lambda p, b, *_: (p, 0, 0, 0)),
            pl.BlockSpec((2, n_taps, WIN, WIN), lambda p, b, *_: (p, 0, 0, 0)),
            pl.BlockSpec((1, two), lambda p, b, *_: (0, p)),
        ],
        out_specs=[
            pl.BlockSpec((2, 1, most, ROWS, WIN), lambda p, b, *_: (p, b, 0, 0, 0)),
            pl.BlockSpec((ROWS, two), lambda p, b, *_: (b, p)),
            pl.BlockSpec((ROWS, two), lambda p, b, *_: (b, p)),
        ],
        scratch_shapes=[
            pltpu.VMEM((HALO + length, two), BF16),
            pltpu.VMEM((TOP + length + HALO, two), BF16),
            pltpu.VMEM((TOP + length + HALO, two), BF16),
            pltpu.VMEM((2, most, ROWS, WIN), F32),
        ],
    )
    return pl.pallas_call(
        functools.partial(forward_kernel, n_taps, key_half, most),
        grid_spec=grid_spec,
        out_shape=[
            jax.ShapeDtypeStruct((heads, blocks, most, ROWS, WIN), F32),
            jax.ShapeDtypeStruct((length, heads * PAD_DIM), F32),
            jax.ShapeDtypeStruct((length, heads * PAD_DIM), BF16),
        ],
        compiler_params=pltpu.CompilerParams(vmem_limit_bytes=40 << 20),
        name="attend_forward",
    )(counts, mix, proj, proj, proj, start, t_hi, t_lo, gain)


def backward_kernel(
    n_taps, key_half, most, count_ref, mix_ref, q_ref, k_ref, v_ref, start_ref, t_back_ref, gain_ref,
    probs_ref, heads_ref, grad_ref, dq_ref, dk_ref, dv_ref, gain_grad_ref, tap_ref, mix_grad_ref,
    qs, ks, vs, dq_sum, dk_sum, dv_sum, taps, inputs, tap_sum, mixed_grad,
):
    pair = pl.program_id(0)
    block = pl.program_id(1)
    length = q_ref.shape[0]
    scale = HEAD_DIM ** (-0.5)

    @pl.when(block == 0)
    def _():
        fill_padded(qs, q_ref, HALO, length)
        fill_padded(ks, k_ref, TOP, length)
        fill_padded(vs, v_ref, TOP, length)
        dq_sum[...] = jnp.zeros_like(dq_sum)
        dk_sum[...] = jnp.zeros_like(dk_sum)
        dv_sum[...] = jnp.zeros_like(dv_sum)
        tap_sum[...] = jnp.zeros_like(tap_sum)
        gain_grad_ref[...] = jnp.zeros_like(gain_grad_ref)
        mix_grad_ref[...] = jnp.zeros_like(mix_grad_ref)

    row0 = pl.multiple_of(block * ROWS, ROWS)

    def body(n):
        grads = []
        for h in range(2):
            cols = slice(h * PAD_DIM, (h + 1) * PAD_DIM)
            out = heads_ref[:, cols]
            factor = lax.rsqrt(jnp.sum(out * out, axis=-1, keepdims=True) * (1.0 / HEAD_DIM) + EPS)
            unit = out * factor
            grad = grad_ref[:, cols]
            gain_grad_ref[:, cols] += jnp.sum(grad * unit, axis=0, keepdims=True)
            scaled = grad * gain_ref[:, cols]
            inner = jnp.sum(scaled * unit, axis=-1, keepdims=True) * (1.0 / HEAD_DIM)
            grads.append((factor * (scaled - unit * inner)).astype(BF16))
        lane = lax.broadcasted_iota(jnp.int32, (ROWS, WIN), 1)
        own = (lane >= OWN) & (lane < WIN - OWN)
        inner = [[None, None], [None, None]]
        for k in range(n):
            base = row0 + ROWS - STEP * (k + 1) - OWN
            at = pl.multiple_of(TOP + base, 16)
            probs = [jnp.where(own, probs_ref[s, 0, k], 0.0) for s in range(2)]
            for h in range(2):
                cols = pl.ds(h * PAD_DIM, PAD_DIM)
                grad_mixed = dot_nt(grads[h], vs[pl.ds(at, WIN), cols])
                mixed_grad[h, k] = grad_mixed
                for s in range(2):
                    part = jnp.sum(grad_mixed * probs[s], axis=-1, keepdims=True)
                    inner[h][s] = part if inner[h][s] is None else inner[h][s] + part
                mixed = (
                    mix_ref[2 * pair + h, 0] * probs[0] + mix_ref[2 * pair + h, 1] * probs[1]
                ).astype(BF16)
                dv_sum[pl.ds(at, WIN), cols] += dot_tn(mixed, grads[h])
        for h in range(2):
            for s in range(2):
                row = 2 * h + s
                mix_grad_ref[0, row : row + 1, :] += jnp.broadcast_to(
                    jnp.sum(inner[h][s], axis=0, keepdims=True), (1, PAD_DIM)
                )
        start = start_ref[pl.ds(row0, EXT), :]
        place = row_numbers(row0 - HALO, EXT)
        for s in range(2):
            cols = pl.ds(s * PAD_DIM, PAD_DIM)
            mix0 = mix_ref[2 * pair, s]
            mix1 = mix_ref[2 * pair + 1, s]
            delta = mix0 * inner[0][s] + mix1 * inner[1][s]
            query = qs[pl.ds(row0, EXT), cols]
            for k in range(n):
                base = row0 + ROWS - STEP * (k + 1) - OWN
                at = pl.multiple_of(TOP + base, 16)
                keys = ks[pl.ds(at, WIN), cols]
                mine = lanes_between(
                    jnp.maximum(start - base, OWN), jnp.minimum(place - base, WIN - OWN - 1), WIN
                )
                grad_prob = mix0 * mixed_grad[0, k] + mix1 * mixed_grad[1, k]
                grad_logit = probs_ref[s, 0, k] * (grad_prob - delta)
                grown = jnp.concatenate([jnp.zeros((HALO, WIN), F32), grad_logit], axis=0)
                for a in range(n_taps):
                    moved = grown if a == 0 else pltpu.roll(grown, EXT - a, 0)
                    taps[k * EXT : (k + 1) * EXT, a * WIN : (a + 1) * WIN] = moved.astype(BF16)
                grad_masked = dot_nn(taps[k * EXT : (k + 1) * EXT, :], t_back_ref[s])
                grad_score = jnp.where(mine, grad_masked * scale, 0.0).astype(BF16)
                dq_sum[pl.ds(row0, EXT), cols] += dot_nn(grad_score, keys)
                dk_sum[pl.ds(at, WIN), cols] += dot_tn(grad_score, query)
                raw = dot_nt(query, keys)
                inputs[k * EXT : (k + 1) * EXT, :] = jnp.where(mine, raw * scale, 0.0).astype(BF16)
            tap_sum[s] += dot_tn(inputs[0 : n * EXT, :], taps[0 : n * EXT, :])

    for n in range(1, most + 1):
        pl.when(count_ref[block] == n)(functools.partial(body, n))

    @pl.when(block == pl.num_programs(1) - 1)
    def _():
        dq_ref[...] = dq_sum[HALO : HALO + length, :].astype(BF16)
        dk_ref[...] = dk_sum[TOP : TOP + length, :].astype(BF16)
        dv_ref[...] = dv_sum[TOP : TOP + length, :].astype(BF16)
        row = lax.broadcasted_iota(jnp.int32, (WIN, WIN), 0)
        lane = lax.broadcasted_iota(jnp.int32, (WIN, WIN), 1)
        for s in range(2):
            for a in range(n_taps):
                whole = tap_sum[s, :, a * WIN : (a + 1) * WIN]
                for b in range(2 * key_half + 1):
                    part = jnp.where(lane - row == b - key_half, whole, 0.0)
                    part = jnp.sum(part, axis=0, keepdims=True)
                    part = jnp.sum(part, axis=1, keepdims=True)
                    at = a * (2 * key_half + 1) + b
                    tap_ref[s, at : at + 1, :] = jnp.broadcast_to(part, (1, PAD_DIM))


def attend_backward(proj, start, counts, t_back, mix, gain, probs, heads_out, grad_grouped):
    length = proj.shape[0]
    heads = probs.shape[0]
    n_taps = t_back.shape[1] // WIN
    pairs = heads // 2
    blocks = length // ROWS
    key_half = 5
    most = windows_most(key_half)
    two = 2 * PAD_DIM
    tap_rows = n_taps * (2 * key_half + 1)
    whole = pl.BlockSpec((length, two), lambda p, b, *_: (0, p))
    grid_spec = pltpu.PrefetchScalarGridSpec(
        num_scalar_prefetch=2,
        grid=(pairs, blocks),
        in_specs=[
            pl.BlockSpec((length, two), lambda p, b, *_: (0, p)),
            pl.BlockSpec((length, two), lambda p, b, *_: (0, pairs + p)),
            pl.BlockSpec((length, two), lambda p, b, *_: (0, 2 * pairs + p)),
            pl.BlockSpec((HALO + length, 1), lambda p, b, *_: (0, 0)),
            pl.BlockSpec((2, n_taps * WIN, WIN), lambda p, b, *_: (p, 0, 0)),
            pl.BlockSpec((1, two), lambda p, b, *_: (0, p)),
            pl.BlockSpec((2, 1, most, ROWS, WIN), lambda p, b, *_: (p, b, 0, 0, 0)),
            pl.BlockSpec((ROWS, two), lambda p, b, *_: (b, p)),
            pl.BlockSpec((ROWS, two), lambda p, b, *_: (b, p)),
        ],
        out_specs=[
            whole,
            whole,
            whole,
            pl.BlockSpec((1, two), lambda p, b, *_: (0, p)),
            pl.BlockSpec((2, tap_rows, PAD_DIM), lambda p, b, *_: (p, 0, 0)),
            pl.BlockSpec((1, 4, PAD_DIM), lambda p, b, *_: (p, 0, 0)),
        ],
        scratch_shapes=[
            pltpu.VMEM((HALO + length, two), BF16),
            pltpu.VMEM((TOP + length + HALO, two), BF16),
            pltpu.VMEM((TOP + length + HALO, two), BF16),
            pltpu.VMEM((HALO + length, two), F32),
            pltpu.VMEM((TOP + length + HALO, two), F32),
            pltpu.VMEM((TOP + length + HALO, two), F32),
            pltpu.VMEM((most * EXT, n_taps * WIN), BF16),
            pltpu.VMEM((most * EXT, WIN), BF16),
            pltpu.VMEM((2, WIN, n_taps * WIN), F32),
            pltpu.VMEM((2, most, ROWS, WIN), F32),
        ],
    )
    return pl.pallas_call(
        functools.partial(backward_kernel, n_taps, key_half, most),
        grid_spec=grid_spec,
        out_shape=[
            jax.ShapeDtypeStruct((length, heads * PAD_DIM), BF16),
            jax.ShapeDtypeStruct((length, heads * PAD_DIM), BF16),
            jax.ShapeDtypeStruct((length, heads * PAD_DIM), BF16),
            jax.ShapeDtypeStruct((1, heads * PAD_DIM), F32),
            jax.ShapeDtypeStruct((heads, tap_rows, PAD_DIM), F32),
            jax.ShapeDtypeStruct((pairs, 4, PAD_DIM), F32),
        ],
        compiler_params=pltpu.CompilerParams(vmem_limit_bytes=48 << 20),
        name="attend_backward",
    )(counts, mix, proj, proj, proj, start, t_back, gain, probs, heads_out, grad_grouped)


MESH_ID = pl.DeviceIdType.MESH


def ring_place(member, n):
    z, y = member // 2, member % 2
    return (1 - y) * z + y * (n - 1 - z)


def ring_member(place, n):
    upper = place // (n // 2)
    return (1 - upper) * 2 * place + upper * (2 * (n - 1 - place) + 1)


def ring_kernel(n, count, *refs):
    ins, outs, slots = refs[:count], refs[count : 2 * count], refs[2 * count : 3 * count]
    rs_send, rs_recv, ag_send, ag_recv = refs[3 * count :]
    place = ring_place(lax.axis_index("dp"), n)
    to = (
        ring_member(lax.rem(place + 1, n), n),
        ring_member(lax.rem(place + n - 1, n), n),
    )
    barrier = pltpu.get_barrier_semaphore()
    for peer in to:
        pl.semaphore_signal(barrier, inc=1, device_id={"dp": peer}, device_id_type=MESH_ID)
    pl.semaphore_wait(barrier, 2)

    def chunk(way, back):
        return lax.rem(place - back + 2 * n if way == 0 else place + back, n)

    def sum_copy(way, k, s, src):
        return pltpu.make_async_remote_copy(
            src_ref=src,
            dst_ref=slots[k].at[way, s],
            send_sem=rs_send.at[way, k, s],
            recv_sem=rs_recv.at[way, k, s],
            device_id={"dp": to[way]},
            device_id_type=MESH_ID,
        )

    def share_copy(way, k, s, c):
        return pltpu.make_async_remote_copy(
            src_ref=outs[k].at[c, way],
            dst_ref=outs[k].at[c, way],
            send_sem=ag_send.at[way, k, s],
            recv_sem=ag_recv.at[way, k, s],
            device_id={"dp": to[way]},
            device_id_type=MESH_ID,
        )

    def add(way, k, s, c, dst):
        total = slots[k][way, s].astype(F32) + ins[k][c, way].astype(F32)
        dst[...] = total.astype(dst.dtype)

    both = [(k, way) for k in range(count) for way in range(2)]
    for k, way in both:
        sum_copy(way, k, 0, ins[k].at[chunk(way, 1), way]).start()

    def sum_step(s, carry):
        for k, way in both:
            sum_copy(way, k, s, slots[k].at[way, s]).wait_recv()
            add(way, k, s, chunk(way, 2 + s), slots[k].at[way, s])
            sum_copy(way, k, s + 1, slots[k].at[way, s]).start()
        return carry

    lax.fori_loop(0, n - 2, sum_step, 0)
    for k, way in both:
        sum_copy(way, k, n - 2, slots[k].at[way, n - 2]).wait_recv()
        add(way, k, n - 2, place, outs[k].at[place, way])
        share_copy(way, k, 0, place).start()

    def share_step(s, carry):
        for k, way in both:
            share_copy(way, k, s, chunk(way, s + 1)).wait_recv()
            share_copy(way, k, s + 1, chunk(way, s + 1)).start()
        return carry

    lax.fori_loop(0, n - 2, share_step, 0)
    for k, way in both:
        share_copy(way, k, n - 2, chunk(way, n - 1)).wait_recv()

    def drain(s, carry):
        for k, way in both:
            sum_copy(way, k, s, slots[k].at[way, s]).wait_send()
            share_copy(way, k, s, place).wait_send()
        return carry

    lax.fori_loop(0, n - 1, drain, 0)


def ring_sum(arrays, collective_id):
    n = lax.axis_size("dp")
    split = [a.reshape(n, 2, -1, a.shape[-1]) for a in arrays]
    count = len(arrays)
    vmem = pl.BlockSpec(memory_space=pltpu.VMEM)
    outs = pl.pallas_call(
        functools.partial(ring_kernel, n, count),
        out_shape=[jax.ShapeDtypeStruct(a.shape, a.dtype) for a in split],
        in_specs=[vmem] * count,
        out_specs=[vmem] * count,
        scratch_shapes=[pltpu.VMEM((2, n - 1) + a.shape[2:], a.dtype) for a in split]
        + [pltpu.SemaphoreType.DMA((2, count, n - 1))] * 4,
        compiler_params=pltpu.CompilerParams(
            collective_id=collective_id, has_side_effects=True, vmem_limit_bytes=60 << 20
        ),
        name="ring_sum",
    )(*split)
    return [o.reshape(a.shape) for o, a in zip(outs, arrays)]


def pack_small(arrays, n):
    flat = jnp.concatenate([a.reshape(-1) for a in arrays])
    unit = 2 * n * 8 * 128
    return jnp.pad(flat, (0, -flat.size % unit)).reshape(-1, 128)


def unpack_small(packed, arrays):
    flat, found, at = packed.reshape(-1), [], 0
    for a in arrays:
        found.append(flat[at : at + a.size].reshape(a.shape))
        at += a.size
    return found


def banded(kernel, back):
    half = kernel.shape[2] // 2
    row = lax.broadcasted_iota(jnp.int32, (WIN, WIN), 0)
    lane = lax.broadcasted_iota(jnp.int32, (WIN, WIN), 1)
    apart = (row - lane if back else lane - row) + half
    full = jnp.zeros(kernel.shape[:2] + (WIN, WIN), F32)
    for b in range(kernel.shape[2]):
        full = jnp.where(apart == b, kernel[:, :, b][:, :, None, None], full)
    return full


def pad_heads(array, axis):
    shape = array.shape
    heads = shape[axis] // HEAD_DIM
    split = array.reshape(shape[:axis] + (heads, HEAD_DIM) + shape[axis + 1 :])
    widths = [(0, 0)] * split.ndim
    widths[axis + 1] = (0, PAD_DIM - HEAD_DIM)
    return jnp.pad(split, widths).reshape(shape[:axis] + (heads * PAD_DIM,) + shape[axis + 1 :])


def cut_heads(array, axis):
    shape = array.shape
    heads = shape[axis] // PAD_DIM
    split = array.reshape(shape[:axis] + (heads, PAD_DIM) + shape[axis + 1 :])
    cut = lax.slice_in_dim(split, 0, HEAD_DIM, axis=axis + 1)
    return cut.reshape(shape[:axis] + (heads * HEAD_DIM,) + shape[axis + 1 :])


def windows_needed(start, key_half):
    length = start.shape[0]
    first = start[::ROWS]
    row0 = jnp.arange(0, length, ROWS, dtype=jnp.int32)
    count = jnp.ones_like(first)
    for k in range(1, windows_most(key_half)):
        count = count + (first - key_half < row0 + ROWS - STEP * k).astype(jnp.int32)
    return count


def on_device(
    tokens, segments, attn_gain, w_qkv, kq_kernel, head_mix, group_gain, w_out, mlp_gain, w_gate_up,
    w_down, cotangent,
):
    rows_here, local_width = tokens.shape
    seq_count, length = segments.shape
    heads_here = local_width // HEAD_DIM
    n_taps, key_taps = kq_kernel.shape[1:]
    key_half = key_taps // 2

    t_full = banded(kq_kernel, False)
    t_hi = t_full.astype(BF16)
    t_lo = (t_full - t_hi.astype(F32)).astype(BF16)
    t_back = banded(kq_kernel, True).astype(BF16).reshape(heads_here, n_taps * WIN, WIN)
    w_proj = pad_heads(w_qkv, 2).transpose(1, 0, 2).reshape(w_qkv.shape[1], -1)
    w_out_pad = pad_heads(w_out, 0)
    gain_heads = pad_heads(group_gain.astype(F32), 0)[None]
    starts, counts = [], []
    for n in range(seq_count):
        seg = segments[n]
        start = jnp.sum((seg[None, :] < seg[:, None]).astype(jnp.int32), axis=1)
        counts.append(windows_needed(start, key_half))
        starts.append(jnp.pad(start, (HALO, 0), constant_values=1 << 20)[:, None])

    gathered = lax.all_gather(tokens, "tensor", axis=1, tiled=True)
    gain_one = lax.all_gather(attn_gain, "tensor", axis=0, tiled=True).astype(F32)
    gain_two = lax.all_gather(mlp_gain, "tensor", axis=0, tiled=True).astype(F32)
    full_cot = lax.all_gather(cotangent, "tensor", axis=1, tiled=True)

    resid = gathered.astype(F32)
    full_width = resid.shape[1]
    scale_one = lax.rsqrt(jnp.mean(resid * resid, axis=-1, keepdims=True) + EPS)
    unit_one = resid * scale_one
    normed_one = (unit_one * gain_one).astype(BF16)
    proj = jnp.dot(normed_one, w_proj, preferred_element_type=F32).astype(BF16)

    kept = []
    for n in range(seq_count):
        rows = slice(n * length, (n + 1) * length)
        kept.append(
            attend_forward(proj[rows], starts[n], counts[n], t_hi, t_lo, head_mix, gain_heads)
        )
    grouped = jnp.concatenate([one[2] for one in kept], axis=0)
    attn_part = jnp.dot(grouped, w_out_pad, preferred_element_type=F32).astype(BF16)
    attn_local = lax.psum_scatter(attn_part, "tensor", scatter_dimension=1, tiled=True).astype(F32)
    hidden_local = tokens.astype(F32) + attn_local
    hidden = lax.all_gather(hidden_local.astype(BF16), "tensor", axis=1, tiled=True).astype(F32)
    scale_two = lax.rsqrt(jnp.mean(hidden * hidden, axis=-1, keepdims=True) + EPS)
    unit_two = hidden * scale_two
    normed_two = (unit_two * gain_two).astype(BF16)

    grad_act = dot_nt(full_cot, w_down)
    gate = jnp.dot(normed_two, w_gate_up[0], preferred_element_type=F32)
    up = jnp.dot(normed_two, w_gate_up[1], preferred_element_type=F32)
    sigmoid = jax.nn.sigmoid(gate)
    swish = gate * sigmoid
    act = (swish * up).astype(BF16)
    grad_gate = (grad_act * up * sigmoid * (1.0 + gate * (1.0 - sigmoid))).astype(BF16)
    grad_up = (grad_act * swish).astype(BF16)
    grad_two_part = dot_nt(grad_gate, w_gate_up[0]) + dot_nt(grad_up, w_gate_up[1])
    grad_two_local = lax.psum_scatter(
        grad_two_part.astype(BF16), "tensor", scatter_dimension=1, tiled=True
    ).astype(F32)
    inner_two = lax.psum(
        jnp.sum(grad_two_part * gain_two * unit_two, axis=-1, keepdims=True), "tensor"
    )
    unit_two_local = hidden_local * scale_two
    grad_gain_two = jnp.sum(grad_two_local * unit_two_local, axis=0)
    grad_hidden_local = cotangent.astype(F32) + scale_two * (
        grad_two_local * mlp_gain.astype(F32) - unit_two_local * (inner_two / full_width)
    )
    grad_attn = lax.all_gather(grad_hidden_local.astype(BF16), "tensor", axis=1, tiled=True)

    mlp_part = jnp.dot(act, w_down, preferred_element_type=F32).astype(BF16)
    mlp_local = lax.psum_scatter(mlp_part, "tensor", scatter_dimension=1, tiled=True).astype(F32)
    layer_out = (hidden_local + mlp_local).astype(BF16)
    grad_down = dot_tn(act, full_cot).astype(BF16)
    grad_gate_up = jnp.stack([dot_tn(normed_two, grad_gate), dot_tn(normed_two, grad_up)]).astype(BF16)
    grad_w_out = cut_heads(dot_tn(grouped, grad_attn).astype(BF16), 0)

    grad_grouped = dot_nt(grad_attn, w_out_pad)
    parts = []
    for n in range(seq_count):
        rows = slice(n * length, (n + 1) * length)
        parts.append(
            attend_backward(
                proj[rows], starts[n], counts[n], t_back, head_mix, gain_heads, kept[n][0], kept[n][1],
                grad_grouped[rows],
            )
        )
    grad_proj = jnp.concatenate(
        [jnp.concatenate([cut_heads(one[c], 1) for c in range(3)], axis=1) for one in parts], axis=0
    )
    grad_group_gain = sum(cut_heads(one[3][0], 0) for one in parts)
    grad_kernel = sum(one[4][:, :, 0] for one in parts).reshape(heads_here, n_taps, key_taps)
    grad_mix = sum(one[5][:, :, 0] for one in parts).reshape(heads_here, 2)

    w_flat = w_qkv.transpose(1, 0, 2).reshape(full_width, 3 * local_width)
    grad_qkv = dot_tn(normed_one, grad_proj).astype(BF16)
    grad_qkv = grad_qkv.reshape(full_width, 3, local_width).transpose(1, 0, 2)
    grad_one_part = dot_nt(grad_proj, w_flat)
    grad_one = lax.psum_scatter(
        grad_one_part.astype(BF16), "tensor", scatter_dimension=1, tiled=True
    ).astype(F32)
    inner_one = lax.psum(
        jnp.sum(grad_one_part * gain_one * unit_one, axis=-1, keepdims=True), "tensor"
    )
    unit_local = tokens.astype(F32) * scale_one
    tokens_grad = grad_hidden_local + scale_one * (
        grad_one * attn_gain.astype(F32) - unit_local * (inner_one / full_width)
    )
    grad_gain_one = jnp.sum(grad_one * unit_local, axis=0)
    small = (grad_gain_one, grad_kernel, grad_mix, grad_group_gain, grad_gain_two)
    grad_gate_up, grad_qkv, grad_down, grad_w_out, packed = ring_sum(
        (grad_gate_up, grad_qkv, grad_down, grad_w_out, pack_small(small, lax.axis_size("dp"))), 0
    )
    grad_gain_one, grad_kernel, grad_mix, grad_group_gain, grad_gain_two = unpack_small(packed, small)
    return (
        layer_out,
        tokens_grad,
        grad_gain_one,
        grad_qkv.astype(F32),
        grad_kernel,
        grad_mix,
        grad_group_gain,
        grad_w_out.astype(F32),
        grad_gain_two,
        grad_gate_up.astype(F32),
        grad_down.astype(F32),
    )


def solution(mesh):
    in_specs = (
        P("dp", "tensor"),
        P("dp", None),
        P("tensor"),
        P(None, None, "tensor"),
        P("tensor", None, None),
        P("tensor", None),
        P("tensor"),
        P("tensor", None),
        P("tensor"),
        P(None, None, "tensor"),
        P("tensor", None),
        P("dp", "tensor"),
    )
    out_specs = (
        P("dp", "tensor"),
        P("dp", "tensor"),
        P("tensor"),
        P(None, None, "tensor"),
        P("tensor", None, None),
        P("tensor", None),
        P("tensor"),
        P("tensor", None),
        P("tensor"),
        P(None, None, "tensor"),
        P("tensor", None),
    )
    return jax.shard_map(
        on_device, mesh=mesh, in_specs=in_specs, out_specs=out_specs, check_vma=False
    )
```

time: 3090 us -> 803 us (0.26)
  other arithmetic: 2250 us -> 67.3 us
  Pallas kernels: 0 us -> 395 us
  local copies, waits for them, and re-layouts: 249 us -> 80.6 us
  matrix products: 276 us -> 109 us
  waiting for transfers between devices: 232 us -> 106 us
  blocking collectives: 55.1 us -> 22.9 us
    reduce_max x1 -> x0, other arithmetic: 755 us -> none  [attend_forward(): peak = jnp.max(logits, axis=-1, keepdims=True)]
    convert_element_type x9 -> x12, other arithmetic: 786 us -> 51.9 us  [the longest x1 14.6 us: on_device(): t_lo = (t_full - t_hi.astype(F32)).astype(BF16)]
    reduce_sum x7 -> x2, other arithmetic: 559 us -> 5.26 us  [the longest x1 3.85 us: on_device(): grad_gain_two = jnp.sum(grad_two_local * unit_two_local, axis=0)]
    pallas_call x0 -> x3, Pallas kernels: none -> 395 us  [the longest x1 289 us: ring_sum(): pl.pallas_call(functools.partial(ring_kernel, n, count), out_shape=[jax.S...]
    psum x3 -> x0, waiting for transfers between devices: 211 us -> none  [the longest x1 111 us: on_device(): attn = lax.psum(attn_part, 'tensor')]
    dot_general x19 -> x15, matrix products: 276 us -> 109 us  [the longest x5 39.4 us: dot_nt(): lax.dot_general(a, b, (((1,), (1,)), ((), ())), preferred_element_type=F32)]
    sub x1 -> x0, other arithmetic: 101 us -> none  [attend_backward(): grad_probs - jnp.sum(grad_probs * probs, axis=-1, keepdims=True)]
    another operation x70 -> x2, local copies, waits for them, and re-layouts: 89.3 us -> 0.17 us  [pack_small(): flat = jnp.concatenate([a.reshape(-1) for a in arrays])]
  transfers between devices with their start and end apart: 7 -> 8, of which waited for: 4 -> 5; matrix products, arithmetic and copies ran while one was open for 62% -> 19% of each run, Pallas kernels for 0% -> 8%
where the time goes in v1:
time: 803 us; the launch traced here: 796 us
  Pallas kernels  395 us (49%)
  matrix products  109 us (14%)
  waiting for transfers between devices  106 us (13%)
  local copies, waits for them, and re-layouts  80.6 us (10%)
  other arithmetic  67.3 us (8%)
  blocking collectives  22.9 us (3%)
  between operations  15 us (2%)
    pallas_call x1, Pallas kernels, ring_sum(): pl.pallas_call(functools.partial(ring_kernel, n, count), out_shape=[jax.S...  289 us
    unnamed x12, waiting for transfers between devices  75.7 us
    pallas_call x1, Pallas kernels, attend_backward(): pl.pallas_call(functools.partial(backward_kernel, n_taps, key_half, most)...  65.4 us
    unnamed x120, local copies, waits for them, and re-layouts  45.6 us
    pallas_call x1, Pallas kernels, attend_forward(): pl.pallas_call(functools.partial(forward_kernel, n_taps, key_half, most),...  40.3 us
    dot_general x5, matrix products, dot_nt(): lax.dot_general(a, b, (((1,), (1,)), ((), ())), preferred_element_type=F32)  39.4 us
    dot_general x5, matrix products, dot_tn(): lax.dot_general(a, b, (((0,), (0,)), ((), ())), preferred_element_type=F32)  28.3 us
    all_gather x1, waiting for transfers between devices, on_device(): lax.all_gather(hidden_local.astype(BF16), 'tensor', axis=1, tiled=True)  22.8 us
  transfers between devices with their start and end apart: 8, of which 5 were waited for; matrix products, arithmetic and copies ran while one was open for 19% of the time, Pallas kernels for 8%

profile of v1, /device:TPU:0, one launch (start us, length us, event | category | flops | bytes accessed | tf_op | source)
XLA Modules:
  0.0 795.6 jit_solution(228381818861473689)
XLA Ops:
  10.3 6.1 copy.84
  16.4 6.1 all-gather
  25.0 4.7 pad.21
  31.4 14.6 %subtract_convert_fusion = (bf16[4,6,256,256]{3,2,1,0:T(8,128)(2,1)}, bf16[4,6,256,256]{3,2,1,0:T(8,128)(2,1)}) fusion(f32[4,6]{1,0:T(4,128)S(1)} %bitcast.225, f32[4,6]{1,0:T(4,128)S(1)} %bitcast.223, f32[4,6]{1,0:T(4,128)S(1)} %bitcast.221, f32[4,6]{1,0:T(4,128)S(1)} %bitcast.219, f32[4,6]{1,0:T(4,128)S(1)} %bitcast.217, f32[4,6]{1,0:T(4,128)S(1)} %bitcast.215, ...), kind=kLoop, calls=%fused_computation.17 | loop fusion | flops 39321600 | bytes 7013408 | tf_op jit(solution)/shard_map/convert_element_type | solution.py:532
  46.0 2.7 fusion.8
  48.9 8.0 %convolution_convert_fusion.2.q_ref.k_ref.v_ref = bf16[1024,1536]{1,0:T(8,128)(2,1)S(1)} fusion(bf16[1536,1536]{0,1:T(8,128)(2,1)} %bitcast.157, bf16[1024,1536]{1,0:T(8,128)(2,1)S(1)} %copy-done.19, f32[1536]{0:T(1024)S(1)} %reshape.181, f32[1024]{0:T(1024)S(1)} %add_rsqrt_fusion.1), kind=kOutput, calls=%fused_computation.28 | convolution fusion | flops 4839702528 | bytes 11020288 | tf_op jit(solution)/shard_map/dot_general | solution.py:554
  56.9 40.3 %attend_forward.1 = (f32[4,8,3,128,256]{4,3,2,1,0:T(8,128)}, f32[1024,512]{1,0:T(8,128)S(1)}, bf16[1024,512]{1,0:T(8,128)(2,1)S(1)}) custom-call(s32[8]{0:T(128)S(1)} %fusion.61.count_ref, f32[4,2]{1,0:T(4,128)S(1)} %copy.96.mix_ref, bf16[1024,1536]{1,0:T(8,128)(2,1)S(1)} %convolution_convert_fusion.2.q_ref.k_ref.v_ref, ...), custom_call_target="tpu_custom_call" | custom-call | tf_op jit(solution)/shard_map/attend_forward/pallas_call | solution.py:174
  99.6 3.5 convolution_convert_fusion.1
  103.0 4.6 copy.110
  107.8 42.3 %reduce-scatter.13.cloned.1.call-done = bf16[384,1024]{1,0:T(8,128)(2,1)} async-done(((bf16[1536,1024]{1,0:T(8,128)(2,1)}), bf16[384,1024]{1,0:T(8,128)(2,1)}) %reduce-scatter.13.cloned.1.call-update) | async-done | bytes 786448
  152.3 2.4 fusion.34
  155.5 5.2 all-gather.1
  160.6 22.8 %all-gather.9.cloned.1.call-done = bf16[1024,1536]{1,0:T(8,128)(2,1)} async-done(((bf16[1024,384]{1,0:T(8,128)(2,1)}), bf16[1024,1536]{1,0:T(8,128)(2,1)}) %all-gather.9.cloned.1.call-update) | async-done | bytes 3145744 | tf_op jit(solution)/shard_map/all_gather | solution.py:566
  183.5 2.7 fusion.9
  186.3 18.6 %fusion.19 = f32[1024,1024]{1,0:T(8,128)} fusion(bf16[2,1536,1024]{2,1,0:T(8,128)(2,1)} %param.21, bf16[1024,1536]{1,0:T(8,128)(2,1)S(1)} %copy-done.20, f32[1536]{0:T(1024)S(1)} %reshape.182, f32[1024]{0:T(1024)S(1)} %add_rsqrt_fusion), kind=kOutput, calls=%fused_computation.41 | convolution fusion | flops 3227516928 | bytes 10496000 | tf_op jit(solution)/shard_map/dot_general | solution.py:572
  204.9 5.0 fusion.15
  210.0 3.5 all-gather.11.cloned.1.call-done
  213.5 9.4 %multiply_convert_fusion = (bf16[1024,1024]{1,0:T(8,128)(2,1)S(1)}, bf16[1024,1024]{1,0:T(8,128)(2,1)S(1)}, bf16[1024,1024]{1,0:T(8,128)(2,1)}) fusion(f32[1024,1024]{1,0:T(8,128)} %fusion.19, f32[1024,1024]{1,0:T(8,128)} %fusion.15, bf16[1024,1536]{1,0:T(8,128)(2,1)} %all-gather.11.cloned.1.call-done, bf16[1024,1536]{1,0:T(8,128)(2,1)S(1)} %copy-done), kind=kOutput, calls=%fused_computation.21 | convolution fusion | flops 3236954112 | bytes 20971520 | tf_op jit(solution)/shard_map/dot_general | solution.py:33
  222.9 6.9 fusion.17
  229.8 7.4 fusion.70
  237.3 4.6 copy.114
  242.0 5.9 psum.14
  247.9 32.1 %reduce-scatter.17.cloned.1.call-done = bf16[384,1024]{1,0:T(8,128)(2,1)} async-done(((bf16[1536,1024]{1,0:T(8,128)(2,1)}), bf16[384,1024]{1,0:T(8,128)(2,1)}) %reduce-scatter.17.cloned.1.call-update) | async-done | bytes 786448
  282.3 3.3 fusion.64
  286.1 6.4 convolution_convert_fusion.6
  292.5 4.7 copy.112
  299.6 11.1 %select_convert_fusion.t_back_ref = bf16[4,1536,256]{2,1,0:T(8,128)(2,1)} fusion(bf16[4,1536]{1,0:T(4,128)(2,1)S(1)} %bitcast.192, bf16[4,1536]{1,0:T(4,128)(2,1)S(1)} %bitcast.193, bf16[4,1536]{1,0:T(4,128)(2,1)S(1)} %bitcast.194, bf16[4,1536]{1,0:T(4,128)(2,1)S(1)} %bitcast.195, bf16[4,1536]{1,0:T(4,128)(2,1)S(1)} %bitcast.196, ...), kind=kLoop, calls=%fused_computation.16 | loop fusion | flops 17301504 | bytes 7606272 | tf_op jit(solution)/shard_map/convert_element_type | solution.py:533
  310.7 3.6 all-gather.13.cloned.1.call-done
  314.4 5.5 fusion.73.grad_ref
  319.9 65.4 %attend_backward.1 = (bf16[1024,512]{1,0:T(8,128)(2,1)S(1)}, bf16[1024,512]{1,0:T(8,128)(2,1)S(1)}, bf16[1024,512]{1,0:T(8,128)(2,1)S(1)}, f32[1,512]{1,0:T(1,12...) custom-call(s32[8]{0:T(128)S(1)} %fusion.61.count_ref, f32[4,2]{1,0:T(4,128)S(1)} %copy.96.mix_ref, ...), custom_call_target="tpu_custom_call" | custom-call | tf_op jit(solution)/shard_map/attend_backward/pallas_call | solution.py:343
  388.2 2.4 copy.109
  396.0 10.2 %fusion.7 = (f32[1024]{0:T(1024)S(1)}, bf16[1024,1536]{1,0:T(8,128)(2,1)}) fusion(bf16[1024,1536]{1,0:T(8,128)(2,1)} %all-gather.7.cloned.1.call-done, f32[1536]{0:T(1024)S(1)} %reshape.181, f32[1024]{0:T(1024)S(1)} %add_rsqrt_fusion.1, bf16[1536,1152]{0,1:T(8,128)(2,1)} %bitcast.150, bf16[1024,384]{0,1:T(8,128)(2,1)S(1)} %bitcast.181, ...), kind=kOutput, calls=%fused_computation.12 | convolution fusion | flops 3640392704 | bytes 12204032 | tf_op jit(solution)/shard_map/dot_general | solution.py:33
  406.1 4.7 copy.116
  412.4 6.0 fusion.13
  418.4 4.0 fusion.12
  422.5 3.9 pad_maximum_fusion
  427.7 5.3 convolution_convert_fusion.3
  433.0 2.5 copy.113
  435.5 9.3 %convolution_convert_fusion = bf16[1536,1152]{0,1:T(8,128)(2,1)} fusion(bf16[1024,384]{0,1:T(8,128)(2,1)S(1)} %bitcast.182, bf16[1024,384]{0,1:T(8,128)(2,1)S(1)} %bitcast.184, bf16[1024,384]{0,1:T(8,128)(2,1)S(1)} %bitcast.186, bf16[1024,1536]{1,0:T(8,128)(2,1)} %all-gather.7.cloned.1.call-done, f32[1536]{0:T(1024)S(1)} %reshape.181, ...), kind=kOutput, calls=%fused_computation.4 | convolution fusion | flops 3639017472 | bytes 9054208 | tf_op jit(solution)/shard_map/dot_general | solution.py:37
  444.8 6.1 copy.104
  451.0 3.7 convolution_convert_fusion.7
  456.3 5.8 psum.15
  464.4 3.8 fusion.32
  469.0 288.8 %ring_sum.1 = (bf16[8,2,192,1024]{3,2,1,0:T(8,128)(2,1)}, bf16[8,2,288,384]{3,2,1,0:T(8,128)(2,1)}, bf16[8,2,64,1536]{3,2,1,0:T(8,128)(2,1)}, bf16[8,2,24,1536]{3,2,1,0:T(8,128)(2,1)}, f32[8,2,8,128]{3,2,1,0:T(8,128)}) custom-call(bf16[8,2,192,1024]{3,2,1,0:T(8,128)(2,1)} %bitcast.147, bf16[8,2,288,384]{3,2,1,0:T(8,128)(2,1)} %bitcast.148, ...), custom_call_target="tpu_custom_call" | custom-call | tf_op jit(solution)/shard_map/ring_sum/pallas_call | solution.py:453
  759.9 6.3 slice.117
  766.1 5.5 convert.18
  775.5 9.3 %convert.20 = f32[2,1536,1024]{2,1,0:T(8,128)} convert(bf16[2,1536,1024]{2,1,0:T(8,128)(2,1)} %bitcast.155) | non-fusion elementwise | flops 3145728 | bytes 18874368 | tf_op jit(solution)/shard_map/convert_element_type | solution.py:647
  784.7 3.8 bitcast_convert_fusion
  (210 shorter events, 39.6 us)
Async XLA Ops:
  7.2 206.3 %copy-start = (bf16[1024,1536]{1,0:T(8,128)(2,1)S(1)}, bf16[1024,1536]{1,0:T(8,128)(2,1)}, u32[]{:S(2)}) copy-start(bf16[1024,1536]{1,0:T(8,128)(2,1)} %param.22) | copy-start | bytes 9437188
  7.2 38.8 %all-gather.7.cloned.1.call-start = ((), (), s32[]{:S(2)}) async-start(), calls=%async_computation.4 | async-start | bytes 3932160 | tf_op jit(solution)/shard_map/all_gather | solution.py:544
  7.9 142.1 %reduce-scatter.13.cloned.1.call-start = ((), (), s32[]{:S(2)}) async-start(), calls=%async_computation.8 | async-start | bytes 3932160
  10.3 6.1 copy-start.32
  10.3 13.4 %copy-start.25 = (f32[4,6,11]{2,0,1:T(4,128)S(1)}, f32[4,6,11]{2,0,1:T(4,128)}, u32[]{:S(2)}) copy-start(f32[4,6,11]{2,0,1:T(4,128)} %param.16) | copy-start | bytes 3172
  10.3 14.7 %copy-start.33 = (bf16[384]{0:T(512)(128)(2,1)S(1)}, bf16[384]{0:T(512)(128)(2,1)}, u32[]{:S(2)}) copy-start(bf16[384]{0:T(512)(128)(2,1)} %param.18) | copy-start | bytes 2308
  25.0 4.8 copy-start.27
  46.0 2.8 copy-start.19
  48.9 8.0 %copy-start.3 = (bf16[4,6,256,256]{3,2,1,0:T(8,128)(2,1)S(1)}, bf16[4,6,256,256]{3,2,1,0:T(8,128)(2,1)}, u32[]{:S(2)}) copy-start(bf16[4,6,256,256]{3,2,1,0:T(8,128)(2,1)} %get-tuple-element.74.t_lo_ref) | copy-start | bytes 9437188
  48.9 8.0 %copy-start.4 = (bf16[4,6,256,256]{3,2,1,0:T(8,128)(2,1)S(1)}, bf16[4,6,256,256]{3,2,1,0:T(8,128)(2,1)}, u32[]{:S(2)}) copy-start(bf16[4,6,256,256]{3,2,1,0:T(8,128)(2,1)} %get-tuple-element.75.t_hi_ref) | copy-start | bytes 9437188
  48.9 8.0 %copy-start.5 = (s32[1040,1]{1,0:T(8,128)S(1)}, s32[1040,1]{1,0:T(8,128)}, u32[]{:S(2)}) copy-start(s32[1040,1]{1,0:T(8,128)} %broadcast_in_dim.409.start_ref) | copy-start | bytes 12484
  56.8 40.4 %copy-start.2 = (bf16[1024,1536]{1,0:T(8,128)(2,1)}, bf16[1024,1536]{1,0:T(8,128)(2,1)S(1)}, u32[]{:S(2)}) copy-start(bf16[1024,1536]{1,0:T(8,128)(2,1)S(1)} %convolution_convert_fusion.2.q_ref.k_ref.v_ref) | copy-start | bytes 9437188
  56.9 42.7 %copy-start.24 = (bf16[4,128,1536]{2,1,0:T(8,128)(2,1)S(1)}, bf16[4,128,1536]{2,1,0:T(8,128)(2,1)}, u32[]{:S(2)}) copy-start(bf16[4,128,1536]{2,1,0:T(8,128)(2,1)} %pad.24) | copy-start | bytes 4718596
  97.2 1.4 copy-start.7
  107.7 47.7 %copy-start.31 = (bf16[384]{0:T(512)(128)(2,1)S(1)}, bf16[384]{0:T(512)(128)(2,1)}, u32[]{:S(2)}) copy-start(bf16[384]{0:T(512)(128)(2,1)} %param.20) | copy-start | bytes 2308
  107.7 75.8 %all-gather.9.cloned.1.call-start = ((), (), s32[]{:S(2)}) async-start(), calls=%async_computation.5 | async-start | bytes 3932160 | tf_op jit(solution)/shard_map/all_gather | solution.py:566
  154.8 58.7 %all-gather.11.cloned.1.call-start = ((), (), s32[]{:S(2)}) async-start(), calls=%async_computation.6 | async-start | bytes 3932160 | tf_op jit(solution)/shard_map/all_gather | solution.py:547
  155.4 124.6 %reduce-scatter.17.cloned.1.call-start = ((), (), s32[]{:S(2)}) async-start(), calls=%async_computation.10 | async-start | bytes 3932160
  183.5 2.8 copy-start.20
  183.5 21.5 %slice-start = ((s8[6291456]{0:T(1024)(128)(4,1)}), s8[4194304]{0:T(1024)(128)(4,1)S(1)}, s32[]{:S(2)}) async-start(s8[6291456]{0:T(1024)(128)(4,1)} %bitcast.231), calls=%async_computation.12 | async-start | bytes 8388608
  186.3 18.6 %slice-start.1 = ((s8[6291456]{0:T(1024)(128)(4,1)}), s8[2097152]{0:T(1024)(128)(4,1)S(1)}, s32[]{:S(2)}) async-start(s8[6291456]{0:T(1024)(128)(4,1)} %bitcast.231), calls=%async_computation.13 | async-start | bytes 4194304
  222.9 6.9 copy-start.37
  222.9 6.9 copy-start.35
  222.9 6.9 copy-start.21
  241.9 72.4 %all-gather.13.cloned.1.call-start = ((), (), s32[]{:S(2)}) async-start(), calls=%async_computation.7 | async-start | bytes 3932160 | tf_op jit(solution)/shard_map/all_gather | solution.py:591
  285.7 147.3 %reduce-scatter.15.cloned.1.call-start = ((), (), s32[]{:S(2)}) async-start(), calls=%async_computation.9 | async-start | bytes 3932160
  297.2 164.9 %reduce-scatter.19.cloned.1.call-start = ((), (), s32[]{:S(2)}) async-start(), calls=%async_computation.11 | async-start | bytes 3932160
  310.7 9.1 %copy-start.6 = (s32[1040,1]{1,0:T(8,128)S(1)}, s32[1040,1]{1,0:T(8,128)}, u32[]{:S(2)}) copy-start(s32[1040,1]{1,0:T(8,128)} %broadcast_in_dim.409.start_ref) | copy-start | bytes 12484
  310.7 9.1 %copy-start.8 = (f32[1024,512]{1,0:T(8,128)S(1)}, f32[1024,512]{1,0:T(8,128)}, u32[]{:S(2)}) copy-start(f32[1024,512]{1,0:T(8,128)} %copy-done.7) | copy-start | bytes 6291460
  385.3 1.0 copy-start.9
  386.2 1.0 copy-start.11
  388.2 3.6 copy-start.12
  390.5 4.8 copy-start.10
  396.0 10.2 %copy-start.29 = (bf16[1024,4,96]{0,2,1:T(8,128)(2,1)}, bf16[1024,4,96]{0,2,1:T(8,128)(2,1)S(1)}, u32[]{:S(2)}) copy-start(bf16[1024,4,96]{0,2,1:T(8,128)(2,1)S(1)} %slice.121) | copy-start | bytes 2359300
  410.8 1.6 copy-start.36
  412.4 6.0 copy-start.22
  412.4 6.0 copy-start.38
  422.5 3.9 copy-start.34
  422.5 5.2 copy-start.39
  427.7 7.8 copy-start.28
  427.7 7.8 copy-start.30
  444.8 6.1 copy-start.15
  454.7 9.7 %copy-start.16 = (bf16[1024,384]{1,0:T(8,128)(2,1)S(1)}, bf16[1024,384]{1,0:T(8,128)(2,1)}, u32[]{:S(2)}) copy-start(bf16[1024,384]{1,0:T(8,128)(2,1)} %param.12) | copy-start | bytes 2359300
  454.7 9.7 %copy-start.17 = (bf16[1024,384]{1,0:T(8,128)(2,1)S(1)}, bf16[1024,384]{1,0:T(8,128)(2,1)}, u32[]{:S(2)}) copy-start(bf16[1024,384]{1,0:T(8,128)(2,1)} %copy.111) | copy-start | bytes 2359300
  454.7 9.7 %copy-start.18 = (bf16[1024,384]{1,0:T(8,128)(2,1)S(1)}, bf16[1024,384]{1,0:T(8,128)(2,1)}, u32[]{:S(2)}) copy-start(bf16[1024,384]{1,0:T(8,128)(2,1)} %param.23) | copy-start | bytes 2359300
  766.1 7.6 copy-start.26
  775.5 9.3 %copy-start.23 = (bf16[8,2,64,1536]{3,2,1,0:T(8,128)(2,1)S(1)}, bf16[8,2,64,1536]{3,2,1,0:T(8,128)(2,1)}, u32[]{:S(2)}) copy-start(bf16[8,2,64,1536]{3,2,1,0:T(8,128)(2,1)} %get-tuple-element.38) | copy-start | bytes 9437188
  784.7 3.8 copy-start.1
  (2 other events, 1.9 us)
Sparse Core Ops, SparseCore 0:
  9.6 31.1 all-gather.6
  107.8 42.1 reduce-scatter.12
  154.9 28.5 all-gather.8
  185.0 28.4 all-gather.10
  242.0 37.9 reduce-scatter.16
  285.8 28.4 all-gather.12
  317.5 37.9 reduce-scatter.14
  410.9 42.7 reduce-scatter.18

commit v2 on v1

--- a/solution.py
+++ b/solution.py
@@ -13,6 +13,7 @@
 EPS = 1e-05
 NEG = -1e30
 
+COST = pl.CostEstimate(flops=1 << 20, bytes_accessed=1 << 10, transcendentals=0)
 ROWS = 128
 HALO = 16
 WIN = 256
@@ -59,8 +60,8 @@
 
 
 def forward_kernel(
-    n_taps, key_half, most, count_ref, mix_ref, q_ref, k_ref, v_ref, start_ref, t_hi_ref, t_lo_ref,
-    gain_ref, probs_ref, heads_ref, grouped_ref, qs, ks, vs, logit_ref,
+    n_taps, key_half, most, count_ref, mix_ref, q_ref, k_ref, v_ref, start_ref, base_ref, gain_ref,
+    probs_ref, heads_ref, grouped_ref, qs, ks, vs, logit_ref, t_hi_ref, t_lo_ref,
 ):
     pair = pl.program_id(0)
     block = pl.program_id(1)
@@ -72,6 +73,12 @@
         fill_padded(qs, q_ref, HALO, length)
         fill_padded(ks, k_ref, TOP, length)
         fill_padded(vs, v_ref, TOP, length)
+        for s in range(2):
+            for a in range(n_taps):
+                band = banded(base_ref[s, a : a + 1, :])
+                high = band.astype(BF16)
+                t_hi_ref[s, a] = high
+                t_lo_ref[s, a] = (band - high.astype(F32)).astype(BF16)
 
     row0 = pl.multiple_of(block * ROWS, ROWS)
 
@@ -139,9 +146,9 @@
         pl.when(count_ref[block] == n)(functools.partial(body, n))
 
 
-def attend_forward(proj, start, counts, t_hi, t_lo, mix, gain):
+def attend_forward(proj, start, counts, base, mix, gain):
     length = proj.shape[0]
-    heads, n_taps = t_hi.shape[:2]
+    heads, n_taps = base.shape[:2]
     pairs = heads // 2
     blocks = length // ROWS
     key_half = 5
@@ -155,8 +162,7 @@
             pl.BlockSpec((length, two), lambda p, b, *_: (0, pairs + p)),
             pl.BlockSpec((length, two), lambda p, b, *_: (0, 2 * pairs + p)),
             pl.BlockSpec((HALO + length, 1), lambda p, b, *_: (0, 0)),
-            pl.BlockSpec((2, n_taps, WIN, WIN), lambda p, b, *_: (p, 0, 0, 0)),
-            pl.BlockSpec((2, n_taps, WIN, WIN), lambda p, b, *_: (p, 0, 0, 0)),
+            pl.BlockSpec((2, n_taps, WIN), lambda p, b, *_: (p, 0, 0)),
             pl.BlockSpec((1, two), lambda p, b, *_: (0, p)),
         ],
         out_specs=[
@@ -169,6 +175,8 @@
             pltpu.VMEM((TOP + length + HALO, two), BF16),
             pltpu.VMEM((TOP + length + HALO, two), BF16),
             pltpu.VMEM((2, most, ROWS, WIN), F32),
+            pltpu.VMEM((2, n_taps, WIN, WIN), BF16),
+            pltpu.VMEM((2, n_taps, WIN, WIN), BF16),
         ],
     )
     return pl.pallas_call(
@@ -180,14 +188,15 @@
             jax.ShapeDtypeStruct((length, heads * PAD_DIM), BF16),
         ],
         compiler_params=pltpu.CompilerParams(vmem_limit_bytes=40 << 20),
+        cost_estimate=COST,
         name="attend_forward",
-    )(counts, mix, proj, proj, proj, start, t_hi, t_lo, gain)
+    )(counts, mix, proj, proj, proj, start, base, gain)
 
 
 def backward_kernel(
-    n_taps, key_half, most, count_ref, mix_ref, q_ref, k_ref, v_ref, start_ref, t_back_ref, gain_ref,
-    probs_ref, heads_ref, grad_ref, dq_ref, dk_ref, dv_ref, gain_grad_ref, tap_ref, mix_grad_ref,
-    qs, ks, vs, dq_sum, dk_sum, dv_sum, taps, inputs, tap_sum, mixed_grad,
+    n_taps, key_half, most, count_ref, mix_ref, q_ref, k_ref, v_ref, start_ref, base_ref, gain_ref,
+    probs_ref, heads_ref, grad_ref, dqkv_ref, inner_ref, gain_grad_ref, tap_ref, mix_grad_ref,
+    qs, ks, vs, dq_sum, dk_sum, dv_sum, taps, inputs, tap_sum, mixed_grad, t_back_ref, kept, inner_sum,
 ):
     pair = pl.program_id(0)
     block = pl.program_id(1)
@@ -205,6 +214,9 @@
         tap_sum[...] = jnp.zeros_like(tap_sum)
         gain_grad_ref[...] = jnp.zeros_like(gain_grad_ref)
         mix_grad_ref[...] = jnp.zeros_like(mix_grad_ref)
+        for s in range(2):
+            for a in range(n_taps):
+                t_back_ref[s, a * WIN : (a + 1) * WIN, :] = banded(base_ref[s, a : a + 1, :]).astype(BF16)
 
     row0 = pl.multiple_of(block * ROWS, ROWS)
 
@@ -278,9 +290,22 @@
 
     @pl.when(block == pl.num_programs(1) - 1)
     def _():
-        dq_ref[...] = dq_sum[HALO : HALO + length, :].astype(BF16)
-        dk_ref[...] = dk_sum[TOP : TOP + length, :].astype(BF16)
-        dv_ref[...] = dv_sum[TOP : TOP + length, :].astype(BF16)
+        inner = None
+        sums = ((dq_sum, HALO, q_ref), (dk_sum, TOP, k_ref), (dv_sum, TOP, v_ref))
+        for c, (total, top, given) in enumerate(sums):
+            grad = total[top : top + length, :].astype(BF16)
+            kept[pair, c] = grad
+            part = jnp.sum(grad.astype(F32) * given[...].astype(F32), axis=-1, keepdims=True)
+            inner = part if inner is None else inner + part
+
+        @pl.when(pair == 0)
+        def _():
+            inner_sum[...] = inner
+
+        @pl.when(pair > 0)
+        def _():
+            inner_sum[...] += inner
+
         row = lax.broadcasted_iota(jnp.int32, (WIN, WIN), 0)
         lane = lax.broadcasted_iota(jnp.int32, (WIN, WIN), 1)
         for s in range(2):
@@ -293,18 +318,37 @@
                     at = a * (2 * key_half + 1) + b
                     tap_ref[s, at : at + 1, :] = jnp.broadcast_to(part, (1, PAD_DIM))
 
-
-def attend_backward(proj, start, counts, t_back, mix, gain, probs, heads_out, grad_grouped):
+    pairs = kept.shape[0]
+
+    @pl.when((block == pl.num_programs(1) - 1) & (pair == pairs - 1))
+    def _():
+        width = 2 * pairs * HEAD_DIM
+
+        def rows_out(n, carry):
+            at = pl.ds(pl.multiple_of(n * ROWS, ROWS), ROWS)
+            for c in range(3):
+                heads = [
+                    kept[p, c, at, s * PAD_DIM : s * PAD_DIM + HEAD_DIM]
+                    for p in range(pairs)
+                    for s in range(2)
+                ]
+                dqkv_ref[at, c * width : (c + 1) * width] = jnp.concatenate(heads, axis=1)
+            column = jnp.broadcast_to(inner_sum[at, :], (ROWS, PAD_DIM))
+            inner_ref[pl.ds(n, 1), :] = column.T[0:1, :]
+            return carry
+
+        lax.fori_loop(0, length // ROWS, rows_out, 0)
+
+
+def attend_backward(proj, start, counts, base, mix, gain, probs, heads_out, grad_grouped):
     length = proj.shape[0]
-    heads = probs.shape[0]
-    n_taps = t_back.shape[1] // WIN
+    heads, n_taps = base.shape[:2]
     pairs = heads // 2
     blocks = length // ROWS
     key_half = 5
     most = windows_most(key_half)
     two = 2 * PAD_DIM
     tap_rows = n_taps * (2 * key_half + 1)
-    whole = pl.BlockSpec((length, two), lambda p, b, *_: (0, p))
     grid_spec = pltpu.PrefetchScalarGridSpec(
         num_scalar_prefetch=2,
         grid=(pairs, blocks),
@@ -313,16 +357,15 @@
             pl.BlockSpec((length, two), lambda p, b, *_: (0, pairs + p)),
             pl.BlockSpec((length, two), lambda p, b, *_: (0, 2 * pairs + p)),
             pl.BlockSpec((HALO + length, 1), lambda p, b, *_: (0, 0)),
-            pl.BlockSpec((2, n_taps * WIN, WIN), lambda p, b, *_: (p, 0, 0)),
+            pl.BlockSpec((2, n_taps, WIN), lambda p, b, *_: (p, 0, 0)),
             pl.BlockSpec((1, two), lambda p, b, *_: (0, p)),
             pl.BlockSpec((2, 1, most, ROWS, WIN), lambda p, b, *_: (p, b, 0, 0, 0)),
             pl.BlockSpec((ROWS, two), lambda p, b, *_: (b, p)),
             pl.BlockSpec((ROWS, two), lambda p, b, *_: (b, p)),
         ],
         out_specs=[
-            whole,
-            whole,
-            whole,
+            pl.BlockSpec((length, 3 * heads * HEAD_DIM), lambda p, b, *_: (0, 0)),
+            pl.BlockSpec((length // ROWS, ROWS), lambda p, b, *_: (0, 0)),
             pl.BlockSpec((1, two), lambda p, b, *_: (0, p)),
             pl.BlockSpec((2, tap_rows, PAD_DIM), lambda p, b, *_: (p, 0, 0)),
             pl.BlockSpec((1, 4, PAD_DIM), lambda p, b, *_: (p, 0, 0)),
@@ -338,22 +381,25 @@
             pltpu.VMEM((most * EXT, WIN), BF16),
             pltpu.VMEM((2, WIN, n_taps * WIN), F32),
             pltpu.VMEM((2, most, ROWS, WIN), F32),
+            pltpu.VMEM((2, n_taps * WIN, WIN), BF16),
+            pltpu.VMEM((pairs, 3, length, two), BF16),
+            pltpu.VMEM((length, 1), F32),
         ],
     )
     return pl.pallas_call(
         functools.partial(backward_kernel, n_taps, key_half, most),
         grid_spec=grid_spec,
         out_shape=[
-            jax.ShapeDtypeStruct((length, heads * PAD_DIM), BF16),
-            jax.ShapeDtypeStruct((length, heads * PAD_DIM), BF16),
-            jax.ShapeDtypeStruct((length, heads * PAD_DIM), BF16),
+            jax.ShapeDtypeStruct((length, 3 * heads * HEAD_DIM), BF16),
+            jax.ShapeDtypeStruct((length // ROWS, ROWS), F32),
             jax.ShapeDtypeStruct((1, heads * PAD_DIM), F32),
             jax.ShapeDtypeStruct((heads, tap_rows, PAD_DIM), F32),
             jax.ShapeDtypeStruct((pairs, 4, PAD_DIM), F32),
         ],
         compiler_params=pltpu.CompilerParams(vmem_limit_bytes=48 << 20),
+        cost_estimate=COST,
         name="attend_backward",
-    )(counts, mix, proj, proj, proj, start, t_back, gain, probs, heads_out, grad_grouped)
+    )(counts, mix, proj, proj, proj, start, base, gain, probs, heads_out, grad_grouped)
 
 
 MESH_ID = pl.DeviceIdType.MESH
@@ -369,18 +415,28 @@
     return (1 - upper) * 2 * place + upper * (2 * (n - 1 - place) + 1)
 
 
-def ring_kernel(n, count, *refs):
-    ins, outs, slots = refs[:count], refs[count : 2 * count], refs[2 * count : 3 * count]
-    rs_send, rs_recv, ag_send, ag_recv = refs[3 * count :]
+def ring_peers(n):
     place = ring_place(lax.axis_index("dp"), n)
-    to = (
-        ring_member(lax.rem(place + 1, n), n),
-        ring_member(lax.rem(place + n - 1, n), n),
-    )
-    barrier = pltpu.get_barrier_semaphore()
-    for peer in to:
-        pl.semaphore_signal(barrier, inc=1, device_id={"dp": peer}, device_id_type=MESH_ID)
-    pl.semaphore_wait(barrier, 2)
+    ahead = ring_member(lax.rem(place + 1, n), n)
+    behind = ring_member(lax.rem(place + n - 1, n), n)
+    return place, (ahead, behind)
+
+
+def ring_scratch(arrays, n):
+    return [pltpu.VMEM((2, n - 1) + a.shape[2:], a.dtype) for a in arrays] + [
+        pltpu.SemaphoreType.DMA((2, len(arrays), n - 1))
+    ] * 4
+
+
+def ring_split(array, n):
+    return array.reshape(n, 2, -1, array.shape[-1])
+
+
+def make_ring(n, ins, outs, scratch):
+    count = len(ins)
+    slots = scratch[:count]
+    rs_send, rs_recv, ag_send, ag_recv = scratch[count:]
+    place, to = ring_peers(n)
 
     def chunk(way, back):
         return lax.rem(place - back + 2 * n if way == 0 else place + back, n)
@@ -410,84 +466,554 @@
         dst[...] = total.astype(dst.dtype)
 
     both = [(k, way) for k in range(count) for way in range(2)]
-    for k, way in both:
-        sum_copy(way, k, 0, ins[k].at[chunk(way, 1), way]).start()
-
-    def sum_step(s, carry):
+
+    def start():
         for k, way in both:
-            sum_copy(way, k, s, slots[k].at[way, s]).wait_recv()
-            add(way, k, s, chunk(way, 2 + s), slots[k].at[way, s])
-            sum_copy(way, k, s + 1, slots[k].at[way, s]).start()
+            sum_copy(way, k, 0, ins[k].at[chunk(way, 1), way]).start()
+
+    def tick(now):
+        @pl.when(now < n - 2)
+        def _():
+            for k, way in both:
+                sum_copy(way, k, now, slots[k].at[way, now]).wait_recv()
+                add(way, k, now, chunk(way, 2 + now), slots[k].at[way, now])
+                sum_copy(way, k, now + 1, slots[k].at[way, now]).start()
+
+        @pl.when(now == n - 2)
+        def _():
+            for k, way in both:
+                sum_copy(way, k, n - 2, slots[k].at[way, n - 2]).wait_recv()
+                add(way, k, n - 2, place, outs[k].at[place, way])
+                share_copy(way, k, 0, place).start()
+
+        @pl.when((now > n - 2) & (now < 2 * n - 3))
+        def _():
+            step = now - (n - 1)
+            for k, way in both:
+                share_copy(way, k, step, chunk(way, step + 1)).wait_recv()
+                share_copy(way, k, step + 1, chunk(way, step + 1)).start()
+
+        @pl.when(now == 2 * n - 3)
+        def _():
+            for k, way in both:
+                share_copy(way, k, n - 2, chunk(way, n - 1)).wait_recv()
+
+    def drain():
+        def one(s, carry):
+            for k, way in both:
+                sum_copy(way, k, s, slots[k].at[way, s]).wait_send()
+                share_copy(way, k, s, place).wait_send()
+            return carry
+
+        lax.fori_loop(0, n - 1, one, 0)
+
+    return start, tick, drain
+
+
+def small_rows(size):
+    return -(-size // PAD_DIM)
+
+
+def pack_small(arrays, rows):
+    packed = []
+    for a in arrays:
+        flat = a.reshape(-1)
+        packed.append(jnp.pad(flat, (0, -flat.size % PAD_DIM)).reshape(-1, PAD_DIM))
+    packed = jnp.concatenate(packed, axis=0)
+    return jnp.pad(packed, ((0, rows - packed.shape[0]), (0, 0)))
+
+
+def unpack_small(packed, arrays):
+    found, at = [], 0
+    for a in arrays:
+        rows = small_rows(a.size)
+        found.append(packed[at : at + rows].reshape(-1)[: a.size].reshape(a.shape))
+        at += rows
+    return found
+
+
+CHUNK = 128
+GROUP = 256
+
+
+LIVE = 4
+
+
+def exchange_scratch(steps, width, ranks, share=True):
+    half = ranks // 2
+    shared = [pltpu.VMEM((steps, ranks, CHUNK, width), BF16)] if share else []
+    return [
+        pltpu.VMEM((steps, half, CHUNK, width), BF16),
+        pltpu.VMEM((steps, half, CHUNK, width), BF16),
+        pltpu.VMEM((LIVE, half, CHUNK, width), F32),
+        pltpu.VMEM((steps, CHUNK, width), BF16),
+        pltpu.VMEM((steps, CHUNK, width), BF16),
+        pltpu.SemaphoreType.DMA((5, steps)),
+        pltpu.SemaphoreType.DMA((5, steps)),
+    ] + shared
+
+
+def tensor_peers():
+    me = lax.axis_index("tensor")
+    return me, me + 1 - 2 * lax.rem(me, 2), lax.rem(me + 2, 4)
+
+
+def meet(signals):
+    barrier = pltpu.get_barrier_semaphore()
+    for device in signals:
+        pl.semaphore_signal(barrier, inc=1, device_id=device, device_id_type=MESH_ID)
+    pl.semaphore_wait(barrier, len(signals))
+
+
+def make_exchange(steps, scratch, partial, local, whole=None, between=None):
+    share = whole is not None
+    out_a, in_a, kept, out_b, in_b, send, recv = scratch[:7]
+    full = scratch[7] if share else None
+    many = GROUP // CHUNK
+    me, near, far = tensor_peers()
+
+    def copy(kind, step, src, dst, peer):
+        return pltpu.make_async_remote_copy(
+            src_ref=src,
+            dst_ref=dst,
+            send_sem=send.at[kind, step],
+            recv_sem=recv.at[kind, step],
+            device_id={"tensor": peer},
+            device_id_type=MESH_ID,
+        )
+
+    def cores(step):
+        return copy(0, step, out_a.at[step], in_a.at[step], near)
+
+    def chips(step):
+        return copy(1, step, out_b.at[step], in_b.at[step], far)
+
+    def back_far(step):
+        return copy(2, step, full.at[step, me], full.at[step, me], far)
+
+    def back_near(step):
+        return copy(3, step, full.at[step, me], full.at[step, me], near)
+
+    def pass_near(step):
+        return copy(4, step, full.at[step, far], full.at[step, far], near)
+
+    def tick(now):
+        @pl.when((lax.rem(now, many) == 0) & (now < steps))
+        def _():
+            for n, owner in ((0, near), (1, lax.rem(near + 2, 4))):
+
+                def put(term, n=n):
+                    term = term.astype(BF16)
+                    for m in range(many):
+                        out_a[now + m, n] = term[m * CHUNK : (m + 1) * CHUNK]
+
+                partial(now, owner, put)
+            for m in range(many):
+                cores(now + m).start()
+            for n, owner in ((1, far), (0, me)):
+
+                def put(term, n=n):
+                    for m in range(many):
+                        kept[lax.rem(now + m, LIVE), n] = term[m * CHUNK : (m + 1) * CHUNK]
+
+                partial(now, owner, put)
+
+        if between is not None:
+            between(now)
+
+        @pl.when((now >= 1) & (now < steps + 1))
+        def _():
+            step = now - 1
+            cores(step).wait_recv()
+            out_b[step] = (kept[lax.rem(step, LIVE), 1] + in_a[step, 1].astype(F32)).astype(BF16)
+            chips(step).start()
+
+        @pl.when((now >= 2) & (now < steps + 2))
+        def _():
+            step = now - 2
+            chips(step).wait_recv()
+            total = kept[lax.rem(step, LIVE), 0] + in_a[step, 0].astype(F32) + in_b[step].astype(F32)
+            shared = local(step, total)
+            if share:
+                full[step, me] = shared.astype(BF16)
+                back_far(step).start()
+                back_near(step).start()
+
+        if share:
+
+            @pl.when((now >= 3) & (now < steps + 3))
+            def _():
+                step = now - 3
+                back_far(step).wait_recv()
+                pass_near(step).start()
+
+            @pl.when((now >= 4) & (now < steps + 4))
+            def _():
+                step = now - 4
+                back_near(step).wait_recv()
+                pass_near(step).wait_recv()
+                whole(step, full)
+
+    def drain():
+        def one(step, carry):
+            cores(step).wait_send()
+            chips(step).wait_send()
+            if share:
+                back_far(step).wait_send()
+                back_near(step).wait_send()
+                pass_near(step).wait_send()
+            return carry
+
+        lax.fori_loop(0, steps, one, 0)
+
+    return tick, steps + (4 if share else 2), drain
+
+
+def run_ticks(count, *ticks):
+    def one(now, carry):
+        for tick in ticks:
+            tick(now)
         return carry
 
-    lax.fori_loop(0, n - 2, sum_step, 0)
-    for k, way in both:
-        sum_copy(way, k, n - 2, slots[k].at[way, n - 2]).wait_recv()
-        add(way, k, n - 2, place, outs[k].at[place, way])
-        share_copy(way, k, 0, place).start()
-
-    def share_step(s, carry):
-        for k, way in both:
-            share_copy(way, k, s, chunk(way, s + 1)).wait_recv()
-            share_copy(way, k, s + 1, chunk(way, s + 1)).start()
+    lax.fori_loop(0, count, one, 0)
+
+
+def group_rows(step):
+    return pl.ds(pl.multiple_of(step * CHUNK, CHUNK), GROUP)
+
+
+def owner_cols(owner, width):
+    return pl.ds(pl.multiple_of(owner * width, PAD_DIM), width)
+
+
+def step_rows(step):
+    return pl.ds(pl.multiple_of(step * CHUNK, CHUNK), CHUNK)
+
+
+def attn_exit_kernel(
+    grouped_ref, w_ref, tokens_ref, gain_ref, hidden_local_ref, hidden_ref, normed_ref, *scratch
+):
+    rows, width = tokens_ref.shape
+    ranks = hidden_ref.shape[1] // width
+
+    def partial(step, owner, put):
+        put(dot_nn(grouped_ref[group_rows(step), :], w_ref[:, owner_cols(owner, width)]))
+
+    def local(step, total):
+        hidden = tokens_ref[step_rows(step), :].astype(F32) + total
+        hidden_local_ref[step_rows(step), :] = hidden
+        return hidden
+
+    def whole(step, full):
+        squares = None
+        for n in range(ranks):
+            block = full[step, n]
+            hidden_ref[step_rows(step), n * width : (n + 1) * width] = block
+            block = block.astype(F32)
+            part = jnp.sum(block * block, axis=-1, keepdims=True)
+            squares = part if squares is None else squares + part
+        factor = lax.rsqrt(squares * (1.0 / (ranks * width)) + EPS)
+        for n in range(ranks):
+            cols = slice(n * width, (n + 1) * width)
+            unit = full[step, n].astype(F32) * factor
+            normed_ref[step_rows(step), cols] = (unit * gain_ref[:, cols]).astype(BF16)
+
+    me, near, far = tensor_peers()
+    meet([{"tensor": near}, {"tensor": far}])
+    tick, ticks, drain = make_exchange(rows // CHUNK, scratch, partial, local, whole)
+    run_ticks(ticks, tick)
+    drain()
+
+
+def attn_exit(grouped, w_out_pad, tokens, gain):
+    rows, width = tokens.shape
+    full_width = w_out_pad.shape[1]
+    vmem = pl.BlockSpec(memory_space=pltpu.VMEM)
+    return pl.pallas_call(
+        attn_exit_kernel,
+        out_shape=[
+            jax.ShapeDtypeStruct((rows, width), F32),
+            jax.ShapeDtypeStruct((rows, full_width), BF16),
+            jax.ShapeDtypeStruct((rows, full_width), BF16),
+        ],
+        in_specs=[vmem] * 4,
+        out_specs=[vmem] * 3,
+        scratch_shapes=exchange_scratch(rows // CHUNK, width, full_width // width),
+        compiler_params=pltpu.CompilerParams(
+            collective_id=1, has_side_effects=True, vmem_limit_bytes=48 << 20
+        ),
+        cost_estimate=COST,
+        name="attn_exit",
+    )(grouped, w_out_pad, tokens, gain)
+
+
+def mlp_exit_kernel(
+    gate_ref, up_ref, w_ref, hidden_ref, cot_ref, hidden_local_ref, cot_local_ref, gain_ref, gain_local_ref,
+    grad_attn_ref, grad_hidden_ref, gain_grad_ref, grad_local, *scratch
+):
+    rows, width = cot_local_ref.shape
+    full_width = hidden_ref.shape[1]
+    ranks = full_width // width
+    gain_grad_ref[...] = jnp.zeros_like(gain_grad_ref)
+
+    def partial(step, owner, put):
+        cols = owner_cols(owner, width)
+        at = group_rows(step)
+        put(dot_nt(gate_ref[at, :], w_ref[0, cols, :]) + dot_nt(up_ref[at, :], w_ref[1, cols, :]))
+
+    def local(step, total):
+        grad_local[step_rows(step), :] = total
+        return total
+
+    def whole(step, full):
+        at = step_rows(step)
+        squares, inner = None, None
+        for n in range(ranks):
+            cols = slice(n * width, (n + 1) * width)
+            hidden = hidden_ref[at, cols].astype(F32)
+            part = jnp.sum(hidden * hidden, axis=-1, keepdims=True)
+            squares = part if squares is None else squares + part
+            part = jnp.sum(full[step, n].astype(F32) * gain_ref[:, cols] * hidden, axis=-1, keepdims=True)
+            inner = part if inner is None else inner + part
+        factor = lax.rsqrt(squares * (1.0 / full_width) + EPS)
+        inner = inner * factor * (1.0 / full_width)
+        for n in range(ranks):
+            cols = slice(n * width, (n + 1) * width)
+            unit = hidden_ref[at, cols].astype(F32) * factor
+            grad = full[step, n].astype(F32) * gain_ref[:, cols] - unit * inner
+            grad_attn_ref[at, cols] = (cot_ref[at, cols].astype(F32) + factor * grad).astype(BF16)
+        total = grad_local[at, :]
+        unit = hidden_local_ref[at, :] * factor
+        gain_grad_ref[...] += jnp.sum(total * unit, axis=0, keepdims=True)
+        grad_hidden_ref[at, :] = cot_local_ref[at, :].astype(F32) + factor * (
+            total * gain_local_ref[...] - unit * inner
+        )
+
+    me, near, far = tensor_peers()
+    meet([{"tensor": near}, {"tensor": far}])
+    tick, ticks, drain = make_exchange(rows // CHUNK, scratch, partial, local, whole)
+    run_ticks(ticks, tick)
+    drain()
+
+
+def mlp_exit(grad_gate, grad_up, w_gate_up, hidden, full_cot, hidden_local, cotangent, gain, gain_local):
+    rows, width = hidden_local.shape
+    full_width = hidden.shape[1]
+    vmem = pl.BlockSpec(memory_space=pltpu.VMEM)
+    return pl.pallas_call(
+        mlp_exit_kernel,
+        out_shape=[
+            jax.ShapeDtypeStruct((rows, full_width), BF16),
+            jax.ShapeDtypeStruct((rows, width), F32),
+            jax.ShapeDtypeStruct((1, width), F32),
+        ],
+        in_specs=[vmem] * 9,
+        out_specs=[vmem] * 3,
+        scratch_shapes=[pltpu.VMEM((rows, width), F32)]
+        + exchange_scratch(rows // CHUNK, width, full_width // width),
+        compiler_params=pltpu.CompilerParams(
+            collective_id=2, has_side_effects=True, vmem_limit_bytes=56 << 20
+        ),
+        cost_estimate=COST,
+        name="mlp_exit",
+    )(grad_gate, grad_up, w_gate_up, hidden, full_cot, hidden_local, cotangent, gain, gain_local)
+
+
+def last_exit_kernel(
+    n_ring, count, grad_ref, w_ref, tokens_ref, grad_hidden_ref, factor_ref, inner_ref, gain_ref, act_ref,
+    w_down_ref, hidden_ref, small_ref, *refs,
+):
+    ins, refs = refs[:count], refs[count:]
+    tokens_grad_ref, out_ref, small_sum_ref = refs[:3]
+    outs, refs = refs[3 : 3 + count], refs[3 + count :]
+    gain_grad, mine, all_small, small_send, small_recv = refs[:5]
+    inner_in, inner_sum, inner_col, inner_send, inner_recv = refs[5:10]
+    ring_refs, scratch = refs[10 : 14 + count], refs[14 + count :]
+    rows, width = tokens_ref.shape
+    full_width = w_ref.shape[1]
+    half = rows // CHUNK
+    me, near, far = tensor_peers()
+    here = lax.axis_index("dp")
+    gain_grad[...] = jnp.zeros_like(gain_grad)
+
+    def partial(step, owner, put):
+        cols = owner_cols(owner, width)
+
+        @pl.when(step < half)
+        def _():
+            total = None
+            for c in range(3):
+                term = dot_nt(grad_ref[group_rows(step), c * width : (c + 1) * width], w_ref[c, cols, :])
+                total = term if total is None else total + term
+            put(total)
+
+        @pl.when(step >= half)
+        def _():
+            put(dot_nn(act_ref[group_rows(step - half), :], w_down_ref[:, cols]))
+
+    def between(now):
+        def copy(n, src, peer):
+            return pltpu.make_async_remote_copy(
+                src_ref=src,
+                dst_ref=inner_in.at[n],
+                send_sem=inner_send.at[n],
+                recv_sem=inner_recv.at[n],
+                device_id={"tensor": peer},
+                device_id_type=MESH_ID,
+            )
+
+        @pl.when(now == 0)
+        def _():
+            copy(0, inner_ref, near).start()
+
+        @pl.when(now == 1)
+        def _():
+            copy(0, inner_ref, near).wait()
+            inner_sum[...] = inner_ref[...] + inner_in[0]
+            copy(1, inner_sum, far).start()
+
+        @pl.when(now == 2)
+        def _():
+            copy(1, inner_sum, far).wait()
+            total = (inner_sum[...] + inner_in[1]) * (1.0 / full_width)
+            for n in range(rows // ROWS):
+                line = jnp.broadcast_to(total[n : n + 1, :], (ROWS, ROWS))
+                inner_col[n * ROWS : (n + 1) * ROWS, :] = line.T[:, 0:1]
+
+    def local(step, total):
+        @pl.when(step < half)
+        def _():
+            at = step_rows(step)
+            factor = factor_ref[at, :]
+            unit = tokens_ref[at, :].astype(F32) * factor
+            gain_grad[...] += jnp.sum(total * unit, axis=0, keepdims=True)
+            tokens_grad_ref[at, :] = grad_hidden_ref[at, :] + factor * (
+                total * gain_ref[...] - unit * inner_col[at, :]
+            )
+
+        @pl.when(step >= half)
+        def _():
+            at = step_rows(step - half)
+            out_ref[at, :] = (hidden_ref[at, :] + total).astype(BF16)
+
+    def small_copy(peer, sender):
+        return pltpu.make_async_remote_copy(
+            src_ref=mine,
+            dst_ref=all_small.at[sender],
+            send_sem=small_send.at[peer],
+            recv_sem=small_recv.at[sender],
+            device_id={"dp": peer},
+            device_id_type=MESH_ID,
+        )
+
+    def small_start(now):
+        @pl.when(now == half + 2)
+        def _():
+            mine[...] = small_ref[...]
+            for n in range(width // PAD_DIM):
+                mine[n : n + 1, :] = gain_grad[:, n * PAD_DIM : (n + 1) * PAD_DIM]
+            all_small[here] = mine[...]
+
+            def one(away, carry):
+                small_copy(lax.rem(here + away, n_ring), here).start()
+                return carry
+
+            lax.fori_loop(1, n_ring, one, 0)
+
+    barrier = pltpu.get_barrier_semaphore()
+    for peer in (near, far):
+        pl.semaphore_signal(barrier, inc=1, device_id={"tensor": peer}, device_id_type=MESH_ID)
+
+    def greet(away, carry):
+        peer = lax.rem(here + away, n_ring)
+        pl.semaphore_signal(barrier, inc=1, device_id={"dp": peer}, device_id_type=MESH_ID)
         return carry
 
-    lax.fori_loop(0, n - 2, share_step, 0)
-    for k, way in both:
-        share_copy(way, k, n - 2, chunk(way, n - 1)).wait_recv()
-
-    def drain(s, carry):
-        for k, way in both:
-            sum_copy(way, k, s, slots[k].at[way, s]).wait_send()
-            share_copy(way, k, s, place).wait_send()
+    lax.fori_loop(1, n_ring, greet, 0)
+    pl.semaphore_wait(barrier, 2 + n_ring - 1)
+
+    ring_start, ring_tick, ring_drain = make_ring(n_ring, ins, outs, ring_refs)
+    tick, ticks, drain = make_exchange(2 * half, scratch, partial, local, between=between)
+    ring_start()
+
+    def two(now):
+        for m in range(2):
+            tick(2 * now + m)
+            small_start(2 * now + m)
+
+    run_ticks(max(-(-ticks // 2), 2 * (n_ring - 1)), two, ring_tick)
+
+    def one(away, carry):
+        peer = lax.rem(here + away, n_ring)
+        small_copy(peer, peer).wait()
         return carry
 
-    lax.fori_loop(0, n - 1, drain, 0)
-
-
-def ring_sum(arrays, collective_id):
-    n = lax.axis_size("dp")
-    split = [a.reshape(n, 2, -1, a.shape[-1]) for a in arrays]
-    count = len(arrays)
+    lax.fori_loop(1, n_ring, one, 0)
+
+    def add(n, total):
+        return total + all_small[n]
+
+    small_sum_ref[...] = lax.fori_loop(1, n_ring, add, all_small[0])
+    drain()
+    ring_drain()
+
+
+def last_exit(
+    grad_proj, w_qkv, tokens, grad_hidden, factor, inner, gain, act, w_down, hidden_local, small, sums
+):
+    rows, width = tokens.shape
+    n_ring = lax.axis_size("dp")
+    count = len(sums)
+    split = [ring_split(a, n_ring) for a in sums]
+    gain_rows = width // PAD_DIM
+    need = gain_rows + sum(small_rows(a.size) for a in small)
+    packed = jnp.pad(pack_small(small, need - gain_rows), ((gain_rows, -need % 8), (0, 0)))
     vmem = pl.BlockSpec(memory_space=pltpu.VMEM)
-    outs = pl.pallas_call(
-        functools.partial(ring_kernel, n, count),
-        out_shape=[jax.ShapeDtypeStruct(a.shape, a.dtype) for a in split],
-        in_specs=[vmem] * count,
-        out_specs=[vmem] * count,
-        scratch_shapes=[pltpu.VMEM((2, n - 1) + a.shape[2:], a.dtype) for a in split]
-        + [pltpu.SemaphoreType.DMA((2, count, n - 1))] * 4,
+    steps = 2 * rows // CHUNK
+    tokens_grad, out, packed, *totals = pl.pallas_call(
+        functools.partial(last_exit_kernel, n_ring, count),
+        out_shape=[
+            jax.ShapeDtypeStruct((rows, width), F32),
+            jax.ShapeDtypeStruct((rows, width), BF16),
+            jax.ShapeDtypeStruct(packed.shape, F32),
+        ]
+        + [jax.ShapeDtypeStruct(a.shape, a.dtype) for a in split],
+        in_specs=[vmem] * (11 + count),
+        out_specs=[vmem] * (3 + count),
+        scratch_shapes=[
+            pltpu.VMEM((1, width), F32),
+            pltpu.VMEM(packed.shape, F32),
+            pltpu.VMEM((n_ring,) + packed.shape, F32),
+            pltpu.SemaphoreType.DMA((n_ring,)),
+            pltpu.SemaphoreType.DMA((n_ring,)),
+            pltpu.VMEM((2,) + inner.shape, F32),
+            pltpu.VMEM(inner.shape, F32),
+            pltpu.VMEM((rows, 1), F32),
+            pltpu.SemaphoreType.DMA((2,)),
+            pltpu.SemaphoreType.DMA((2,)),
+        ]
+        + ring_scratch(split, n_ring)
+        + exchange_scratch(steps, width, w_qkv.shape[1] // width, share=False),
         compiler_params=pltpu.CompilerParams(
-            collective_id=collective_id, has_side_effects=True, vmem_limit_bytes=60 << 20
+            collective_id=3, has_side_effects=True, vmem_limit_bytes=62 << 20
         ),
-        name="ring_sum",
-    )(*split)
-    return [o.reshape(a.shape) for o, a in zip(outs, arrays)]
-
-
-def pack_small(arrays, n):
-    flat = jnp.concatenate([a.reshape(-1) for a in arrays])
-    unit = 2 * n * 8 * 128
-    return jnp.pad(flat, (0, -flat.size % unit)).reshape(-1, 128)
-
-
-def unpack_small(packed, arrays):
-    flat, found, at = packed.reshape(-1), [], 0
-    for a in arrays:
-        found.append(flat[at : at + a.size].reshape(a.shape))
-        at += a.size
-    return found
-
-
-def banded(kernel, back):
-    half = kernel.shape[2] // 2
-    row = lax.broadcasted_iota(jnp.int32, (WIN, WIN), 0)
-    lane = lax.broadcasted_iota(jnp.int32, (WIN, WIN), 1)
-    apart = (row - lane if back else lane - row) + half
-    full = jnp.zeros(kernel.shape[:2] + (WIN, WIN), F32)
-    for b in range(kernel.shape[2]):
-        full = jnp.where(apart == b, kernel[:, :, b][:, :, None, None], full)
-    return full
+        cost_estimate=COST,
+        name="last_exit",
+    )(grad_proj, w_qkv, tokens, grad_hidden, factor, inner, gain, act, w_down, hidden_local, packed, *split)
+    gain_grad = packed[:gain_rows].reshape(width)
+    totals = [t.reshape(a.shape) for t, a in zip(totals, sums)]
+    return tokens_grad, gain_grad, out, unpack_small(packed[gain_rows:], small), totals
+
+
+def banded(line):
+    return pltpu.roll(jnp.broadcast_to(line, (WIN, WIN)), 0, 1, stride=1, stride_axis=0)
+
+
+def band_lines(kernel):
+    taps = kernel.shape[2]
+    wide = jnp.pad(kernel, ((0, 0), (0, 0), (0, WIN - taps)))
+    back = jnp.pad(kernel[:, :, ::-1], ((0, 0), (0, 0), (0, WIN - taps)))
+    return jnp.roll(wide, -(taps // 2), axis=2), jnp.roll(back, -(taps // 2), axis=2)
 
 
 def pad_heads(array, axis):
@@ -527,10 +1053,7 @@
     n_taps, key_taps = kq_kernel.shape[1:]
     key_half = key_taps // 2
 
-    t_full = banded(kq_kernel, False)
-    t_hi = t_full.astype(BF16)
-    t_lo = (t_full - t_hi.astype(F32)).astype(BF16)
-    t_back = banded(kq_kernel, True).astype(BF16).reshape(heads_here, n_taps * WIN, WIN)
+    lines, lines_back = band_lines(kq_kernel)
     w_proj = pad_heads(w_qkv, 2).transpose(1, 0, 2).reshape(w_qkv.shape[1], -1)
     w_out_pad = pad_heads(w_out, 0)
     gain_heads = pad_heads(group_gain.astype(F32), 0)[None]
@@ -542,8 +1065,8 @@
         starts.append(jnp.pad(start, (HALO, 0), constant_values=1 << 20)[:, None])
 
     gathered = lax.all_gather(tokens, "tensor", axis=1, tiled=True)
-    gain_one = lax.all_gather(attn_gain, "tensor", axis=0, tiled=True).astype(F32)
-    gain_two = lax.all_gather(mlp_gain, "tensor", axis=0, tiled=True).astype(F32)
+    gains = lax.all_gather(jnp.stack([attn_gain, mlp_gain]), "tensor", axis=1, tiled=True).astype(F32)
+    gain_one, gain_two = gains[0], gains[1]
     full_cot = lax.all_gather(cotangent, "tensor", axis=1, tiled=True)
 
     resid = gathered.astype(F32)
@@ -557,16 +1080,11 @@
     for n in range(seq_count):
         rows = slice(n * length, (n + 1) * length)
         kept.append(
-            attend_forward(proj[rows], starts[n], counts[n], t_hi, t_lo, head_mix, gain_heads)
+            attend_forward(proj[rows], starts[n], counts[n], lines, head_mix, gain_heads)
         )
     grouped = jnp.concatenate([one[2] for one in kept], axis=0)
-    attn_part = jnp.dot(grouped, w_out_pad, preferred_element_type=F32).astype(BF16)
-    attn_local = lax.psum_scatter(attn_part, "tensor", scatter_dimension=1, tiled=True).astype(F32)
-    hidden_local = tokens.astype(F32) + attn_local
-    hidden = lax.all_gather(hidden_local.astype(BF16), "tensor", axis=1, tiled=True).astype(F32)
-    scale_two = lax.rsqrt(jnp.mean(hidden * hidden, axis=-1, keepdims=True) + EPS)
-    unit_two = hidden * scale_two
-    normed_two = (unit_two * gain_two).astype(BF16)
+    grouped, full_cot = lax.optimization_barrier((grouped, full_cot))
+    hidden_local, hidden, normed_two = attn_exit(grouped, w_out_pad, tokens, gain_two[None])
 
     grad_act = dot_nt(full_cot, w_down)
     gate = jnp.dot(normed_two, w_gate_up[0], preferred_element_type=F32)
@@ -576,25 +1094,15 @@
     act = (swish * up).astype(BF16)
     grad_gate = (grad_act * up * sigmoid * (1.0 + gate * (1.0 - sigmoid))).astype(BF16)
     grad_up = (grad_act * swish).astype(BF16)
-    grad_two_part = dot_nt(grad_gate, w_gate_up[0]) + dot_nt(grad_up, w_gate_up[1])
-    grad_two_local = lax.psum_scatter(
-        grad_two_part.astype(BF16), "tensor", scatter_dimension=1, tiled=True
-    ).astype(F32)
-    inner_two = lax.psum(
-        jnp.sum(grad_two_part * gain_two * unit_two, axis=-1, keepdims=True), "tensor"
+    grad_down = dot_tn(act, full_cot).astype(BF16)
+    grad_up_w = dot_tn(normed_two, grad_up).astype(BF16)
+    grad_gate, grad_up_w, grad_down = lax.optimization_barrier((grad_gate, grad_up_w, grad_down))
+    grad_up_w, grad_down = lax.psum((grad_up_w, grad_down), "dp")
+    grad_attn, grad_hidden_local, grad_gain_two = mlp_exit(
+        grad_gate, grad_up, w_gate_up, hidden, full_cot, hidden_local, cotangent, gain_two[None],
+        mlp_gain.astype(F32)[None],
     )
-    unit_two_local = hidden_local * scale_two
-    grad_gain_two = jnp.sum(grad_two_local * unit_two_local, axis=0)
-    grad_hidden_local = cotangent.astype(F32) + scale_two * (
-        grad_two_local * mlp_gain.astype(F32) - unit_two_local * (inner_two / full_width)
-    )
-    grad_attn = lax.all_gather(grad_hidden_local.astype(BF16), "tensor", axis=1, tiled=True)
-
-    mlp_part = jnp.dot(act, w_down, preferred_element_type=F32).astype(BF16)
-    mlp_local = lax.psum_scatter(mlp_part, "tensor", scatter_dimension=1, tiled=True).astype(F32)
-    layer_out = (hidden_local + mlp_local).astype(BF16)
-    grad_down = dot_tn(act, full_cot).astype(BF16)
-    grad_gate_up = jnp.stack([dot_tn(normed_two, grad_gate), dot_tn(normed_two, grad_up)]).astype(BF16)
+    grad_gate_w = dot_tn(normed_two, grad_gate).astype(BF16)
     grad_w_out = cut_heads(dot_tn(grouped, grad_attn).astype(BF16), 0)
 
     grad_grouped = dot_nt(grad_attn, w_out_pad)
@@ -603,37 +1111,29 @@
         rows = slice(n * length, (n + 1) * length)
         parts.append(
             attend_backward(
-                proj[rows], starts[n], counts[n], t_back, head_mix, gain_heads, kept[n][0], kept[n][1],
+                proj[rows], starts[n], counts[n], lines_back, head_mix, gain_heads, kept[n][0], kept[n][1],
                 grad_grouped[rows],
             )
         )
-    grad_proj = jnp.concatenate(
-        [jnp.concatenate([cut_heads(one[c], 1) for c in range(3)], axis=1) for one in parts], axis=0
+    grad_proj = jnp.concatenate([one[0] for one in parts], axis=0)
+    inner_part = jnp.concatenate([one[1] for one in parts], axis=0)
+    grad_group_gain = sum(cut_heads(one[2][0], 0) for one in parts)
+    grad_kernel = sum(one[3][:, :, 0] for one in parts).reshape(heads_here, n_taps, key_taps)
+    grad_mix = sum(one[4][:, :, 0] for one in parts).reshape(heads_here, 2)
+
+    grad_qkv = [
+        dot_tn(normed_one, grad_proj[:, c * local_width : (c + 1) * local_width]).astype(BF16)
+        for c in range(3)
+    ]
+    tokens_grad, grad_gain_one, layer_out, small, sums = last_exit(
+        grad_proj, w_qkv, tokens, grad_hidden_local, scale_one, inner_part, attn_gain.astype(F32)[None],
+        act, w_down, hidden_local, (grad_kernel, grad_mix, grad_group_gain, grad_gain_two[0]),
+        (grad_gate_w, grad_w_out, *grad_qkv),
     )
-    grad_group_gain = sum(cut_heads(one[3][0], 0) for one in parts)
-    grad_kernel = sum(one[4][:, :, 0] for one in parts).reshape(heads_here, n_taps, key_taps)
-    grad_mix = sum(one[5][:, :, 0] for one in parts).reshape(heads_here, 2)
-
-    w_flat = w_qkv.transpose(1, 0, 2).reshape(full_width, 3 * local_width)
-    grad_qkv = dot_tn(normed_one, grad_proj).astype(BF16)
-    grad_qkv = grad_qkv.reshape(full_width, 3, local_width).transpose(1, 0, 2)
-    grad_one_part = dot_nt(grad_proj, w_flat)
-    grad_one = lax.psum_scatter(
-        grad_one_part.astype(BF16), "tensor", scatter_dimension=1, tiled=True
-    ).astype(F32)
-    inner_one = lax.psum(
-        jnp.sum(grad_one_part * gain_one * unit_one, axis=-1, keepdims=True), "tensor"
-    )
-    unit_local = tokens.astype(F32) * scale_one
-    tokens_grad = grad_hidden_local + scale_one * (
-        grad_one * attn_gain.astype(F32) - unit_local * (inner_one / full_width)
-    )
-    grad_gain_one = jnp.sum(grad_one * unit_local, axis=0)
-    small = (grad_gain_one, grad_kernel, grad_mix, grad_group_gain, grad_gain_two)
-    grad_gate_up, grad_qkv, grad_down, grad_w_out, packed = ring_sum(
-        (grad_gate_up, grad_qkv, grad_down, grad_w_out, pack_small(small, lax.axis_size("dp"))), 0
-    )
-    grad_gain_one, grad_kernel, grad_mix, grad_group_gain, grad_gain_two = unpack_small(packed, small)
+    grad_kernel, grad_mix, grad_group_gain, grad_gain_two = small
+    grad_gate_w, grad_w_out, *grad_qkv = sums
+    grad_gate_up = jnp.stack([grad_gate_w, grad_up_w])
+    grad_qkv = jnp.stack(grad_qkv)
     return (
         layer_out,
         tokens_grad,

time: 803 us -> 581 us (0.72)
  waiting for transfers between devices: 106 us -> 10.3 us
  matrix products: 109 us -> 58.1 us
  local copies, waits for them, and re-layouts: 80.6 us -> 31.8 us
  other arithmetic: 67.3 us -> 24.6 us
  Pallas kernels: 395 us -> 425 us
  blocking collectives: 22.9 us -> 6.09 us
    unnamed x12 -> x3, waiting for transfers between devices: 75.7 us -> 1.39 us
    dot_general x5 -> x2, matrix products: 39.4 us -> 7.33 us  [dot_nt(): lax.dot_general(a, b, (((1,), (1,)), ((), ())), preferred_element_type=F32)]
    convert_element_type x8 -> x1, other arithmetic: 31.6 us -> 0.01 us  [on_device(): lax.all_gather(jnp.stack([attn_gain, mlp_gain]), 'tensor', axis=1, tiled=...]
    unnamed x120 -> x81, local copies, waits for them, and re-layouts: 45.6 us -> 17.9 us
    pallas_call x1 -> x3, Pallas kernels: 289 us -> 315 us  [the longest x1 220 us: last_exit(): pl.pallas_call(functools.partial(last_exit_kernel, n_ring, count), out_sh...]
    all_gather x2 -> x0, waiting for transfers between devices: 26.5 us -> none  [the longest x1 22.8 us: on_device(): lax.all_gather(hidden_local.astype(BF16), 'tensor', axis=1, tiled=True)]
    dot_general x1, matrix products: 18.6 us -> 6.83 us  [on_device(): gate = jnp.dot(normed_two, w_gate_up[0], preferred_element_type=F32)]
    psum x2 -> x0, blocking collectives: 11.7 us -> none  [the longest x1 5.9 us: on_device(): lax.psum(jnp.sum(grad_two_part * gain_two * unit_two, axis=-1, keepdims=T...]
  transfers between devices with their start and end apart: 8 -> 3, of which waited for: 5 -> 1; matrix products, arithmetic and copies ran while one was open for 19% -> 12% of each run, Pallas kernels for 8% -> 67%
where the time goes in v2:
time: 581 us; the launch traced here: 571 us
  Pallas kernels  425 us (73%)
  matrix products  58.1 us (10%)
  local copies, waits for them, and re-layouts  31.8 us (5%)
  other arithmetic  24.6 us (4%)
  between operations  14.5 us (2%)
  waiting for transfers between devices  10.3 us (2%)
  blocking collectives  6.09 us (1%)
    pallas_call x1, Pallas kernels, last_exit(): pl.pallas_call(functools.partial(last_exit_kernel, n_ring, count), out_sh...  220 us
    pallas_call x1, Pallas kernels, attend_backward(): pl.pallas_call(functools.partial(backward_kernel, n_taps, key_half, most)...  69.1 us
    pallas_call x1, Pallas kernels, mlp_exit(): pl.pallas_call(mlp_exit_kernel, out_shape=[jax.ShapeDtypeStruct((rows, fu...  52.7 us
    pallas_call x1, Pallas kernels, attn_exit(): pl.pallas_call(attn_exit_kernel, out_shape=[jax.ShapeDtypeStruct((rows, w...  43.1 us
    pallas_call x1, Pallas kernels, attend_forward(): pl.pallas_call(functools.partial(forward_kernel, n_taps, key_half, most),...  40.8 us
    dot_general x7, matrix products, dot_tn(): lax.dot_general(a, b, (((0,), (0,)), ((), ())), preferred_element_type=F32)  29.9 us
    unnamed x81, local copies, waits for them, and re-layouts  17.9 us
  transfers between devices with their start and end apart: 3, of which 1 were waited for; matrix products, arithmetic and copies ran while one was open for 12% of the time, Pallas kernels for 67%

profile of v2, /device:TPU:0, one launch (start us, length us, event | category | flops | bytes accessed | tf_op | source)
XLA Modules:
  0.0 570.7 jit_solution(13783223716780515452)
XLA Ops:
  7.2 0.7 all-gather.3.cloned.1.call-update
  8.0 0.7 all-gather.5.cloned.1.call-update
  8.7 0.7 stack.19
  9.4 0.7 stack.18
  10.1 6.1 %all_gather.10 = bf16[2,1536]{1,0:T(2,128)(2,1)S(1)} all-gather(bf16[2,384]{1,0:T(2,128)(2,1)S(1)} %pad_maximum_fusion.2), channel_id=1, replica_groups=mesh['dp'=8,'tensor'=4] {'tensor'}, dimensions={1}, use_global_device_ids=true | all-gather | bytes 7680 | tf_op jit(solution)/shard_map/all_gather | solution.py:1068
  16.2 1.3 convert_reduce_fusion
  17.6 0.8 copy.49.mix_ref
  18.4 6.1 %copy.42 = bf16[3,1536,384]{1,2,0:T(8,128)(2,1)} copy(bf16[3,1536,384]{2,1,0:T(8,128)(2,1)} %w_ref.3) | data formatting | bytes 7077888 | tf_op args[3]
  24.6 1.0 broadcast_in_dim.13.start_ref
  25.7 4.7 pad.36
  30.5 1.3 pad.41
  32.0 8.9 %all-gather.3.cloned.1.call-done = bf16[1024,1536]{1,0:T(8,128)(2,1)} async-done(((bf16[1024,384]{1,0:T(8,128)(2,1)}), bf16[1024,1536]{1,0:T(8,128)(2,1)}) %all-gather.3.cloned.1.call-update) | async-done | bytes 3145744 | tf_op jit(solution)/shard_map/all_gather | solution.py:1067
  40.9 2.7 fusion
  43.7 7.9 %convolution_convert_fusion.q_ref.k_ref.v_ref = bf16[1024,1536]{1,0:T(8,128)(2,1)S(1)} fusion(bf16[1536,1536]{0,1:T(8,128)(2,1)} %bitcast.72, bf16[1024,1536]{1,0:T(8,128)(2,1)S(1)} %copy-done.17, f32[1536]{0:T(1024)S(1)} %slice_reduce_fusion.1, f32[1024]{0:T(1024)S(1)} %add_rsqrt_fusion), kind=kOutput, calls=%fused_computation.12 | convolution fusion | flops 4839702528 | bytes 11020288 | tf_op jit(solution)/shard_map/dot_general | solution.py:1077
  51.6 40.8 %attend_forward.1 = (f32[4,8,3,128,256]{4,3,2,1,0:T(8,128)}, f32[1024,512]{1,0:T(8,128)S(1)}, bf16[1024,512]{1,0:T(8,128)(2,1)S(1)}) custom-call(s32[8]{0:T(128)S(1)} %fusion.15.count_ref, f32[4,2]{1,0:T(4,128)S(1)} %copy.49.mix_ref, bf16[1024,1536]{1,0:T(8,128)(2,1)S(1)} %convolution_convert_fusion.q_ref.k_ref.v_ref, ...), custom_call_target="tpu_custom_call" | custom-call | flops 1048576 | bytes 1024 | tf_op jit(solution)/shard_map/attend_forward/pallas_call | solution.py:182
  92.4 1.3 copy-done.7
  93.7 0.9 copy-done.9
  94.7 1.1 copy-done.1
  95.8 1.4 copy-done.2
  97.2 1.2 copy-done.10
  98.5 43.1 %attn_exit.1 = (f32[1024,384]{1,0:T(8,128)S(1)}, bf16[1024,1536]{1,0:T(8,128)(2,1)}, bf16[1024,1536]{1,0:T(8,128)(2,1)}) custom-call(bf16[1024,512]{1,0:T(8,128)(2,1)S(1)} %copy-done.10, bf16[512,1536]{1,0:T(8,128)(2,1)S(1)} %bitcast.64, bf16[1024,384]{1,0:T(8,128)(2,1)S(1)} %copy-done.1, f32[1,1536]{1,0:T(1,128)S(1)} %slice.107.gain_ref), custom_call_target="tpu_custom_call" | custom-call | flops 1048576 | bytes 1024 | tf_op jit(solution)/shard_map/attn_exit/pallas_call | solution.py:732
  141.6 6.8 %fusion.4 = f32[1024,1024]{1,0:T(8,128)S(1)} fusion(bf16[1024,1536]{1,0:T(8,128)(2,1)} %get-tuple-element.43, bf16[2,1536,1024]{2,1,0:T(8,128)(2,1)} %w_ref.2), kind=kOutput, calls=%fused_computation.17 | convolution fusion | flops 3221225472 | bytes 10485760 | tf_op jit(solution)/shard_map/dot_general | solution.py:1090
  148.5 3.4 fusion.21
  152.0 6.2 %multiply_convert_fusion = (bf16[1024,1024]{1,0:T(8,128)(2,1)S(1)}, bf16[1024,1024]{1,0:T(8,128)(2,1)}, bf16[1024,1024]{1,0:T(8,128)(2,1)S(1)}) fusion(f32[1024,1024]{1,0:T(8,128)S(1)} %fusion.4, f32[1024,1024]{1,0:T(8,128)S(1)} %fusion.21, bf16[1024,1536]{1,0:T(8,128)(2,1)S(1)} %copy-done.33, bf16[2,1536,1024]{2,1,0:T(8,128)(2,1)S(1)} %bitcast.71), kind=kOutput, calls=%fused_computation.6 | convolution fusion | flops 3236954112 | bytes 20971520 | tf_op jit(solution)/shard_map/dot_general | solution.py:1091
  158.2 4.9 convolution_convert_fusion.3
  163.1 5.0 convolution_convert_fusion.2
  170.1 1.0 copy.51.factor_ref
  171.1 52.7 %mlp_exit.1 = (bf16[1024,1536]{1,0:T(8,128)(2,1)}, f32[1024,384]{1,0:T(8,128)}, f32[1,384]{1,0:T(1,128)}) custom-call(bf16[1024,1024]{1,0:T(8,128)(2,1)} %get-tuple-element.44.gate_ref, bf16[1024,1024]{1,0:T(8,128)(2,1)} %copy-done.22, bf16[2,1536,1024]{2,1,0:T(8,128)(2,1)} %w_ref.2, bf16[1024,1536]{1,0:T(8,128)(2,1)} %get-tuple-element.45.hidden_ref, ...), custom_call_target="tpu_custom_call" | custom-call | flops 1048576 | bytes 1024 | tf_op jit(solution)/shard_map/mlp_exit/pallas_call | solution.py:803
  223.9 3.9 fusion.22.grad_ref
  227.9 69.1 %attend_backward.1 = (bf16[1024,1152]{1,0:T(8,128)(2,1)}, f32[8,128]{1,0:T(8,128)S(1)}, f32[1,512]{1,0:T(1,128)S(1)}, f32[4,66,128]{2,1,0:T(8,128)S(1)}, f32[2,4,128]{2,1,0:T(4,128)S(1)}) custom-call(s32[8]{0:T(128)S(1)} %fusion.15.count_ref, f32[4,2]{1,0:T(4,128)S(1)} %copy.49.mix_ref, bf16[1024,1536]{1,0:T(8,128)(2,1)} %copy-done, ...), custom_call_target="tpu_custom_call" | custom-call | flops 1048576 | bytes 1024 | tf_op jit(solution)/shard_map/attend_backward/pallas_call | solution.py:389
  298.0 4.0 convolution_convert_fusion.4
  302.0 1.1 slice.108
  303.1 0.6 select_maximum_fusion.small_ref
  303.8 5.0 convolution_convert_fusion.7
  308.8 3.1 convolution_convert_fusion.6
  311.9 3.0 convolution_convert_fusion.5
  315.2 4.9 convolution_convert_fusion.1
  320.1 219.6 %last_exit.1 = (f32[1024,384]{1,0:T(8,128)}, bf16[1024,384]{1,0:T(8,128)(2,1)}, f32[16,128]{1,0:T(8,128)}, bf16[8,2,96,1024]{3,2,1,0:T(8,128)(2,1)}, bf16[8,2,24...) custom-call(bf16[1024,1152]{1,0:T(8,128)(2,1)} %get-tuple-element.48, ...), custom_call_target="tpu_custom_call" | custom-call | flops 1048576 | bytes 1024 | tf_op jit(solution)/shard_map/last_exit/pallas_call | solution.py:973
  539.6 1.4 slice_bitcast_fusion
  541.1 0.6 copy.52
  541.7 0.7 slice_reduce_fusion.3
  542.5 0.7 copy.53
  543.1 5.6 maximum_convert_fusion.1
  548.7 1.8 bitcast_convert_fusion
  550.5 5.6 convert_element_type.105
  556.1 5.6 maximum_convert_fusion
  561.7 0.9 copy.58
  562.6 1.1 copy.59
  (106 shorter events, 4.4 us)
Async XLA Ops:
  7.2 33.7 %all-gather.3.cloned.1.call-start = ((), (), s32[]{:S(2)}) async-start(), calls=%async_computation | async-start | bytes 3932160 | tf_op jit(solution)/shard_map/all_gather | solution.py:1067
  7.9 86.8 %all-gather.5.cloned.1.call-start = ((), (), s32[]{:S(2)}) async-start(), calls=%async_computation.1 | async-start | bytes 3932160 | tf_op jit(solution)/shard_map/all_gather | solution.py:1070
  8.7 541.8 %all-reduce.12.cloned.1.call-start = ((), (), s32[]{:S(2)}) async-start(), calls=%async_computation.2 | async-start | bytes 12582912 | tf_op jit(solution)/shard_map/psum | solution.py:1100
  16.2 78.5 %copy-start.12 = (f32[1,1536]{1,0:T(1,128)}, f32[1,1536]{1,0:T(1,128)S(1)}, u32[]{:S(2)}) copy-start(f32[1,1536]{1,0:T(1,128)S(1)} %slice.107.gain_ref) | copy-start | bytes 18436
  18.4 7.2 %copy-start.28 = (f32[4,6,11]{2,0,1:T(4,128)S(1)}, f32[4,6,11]{2,0,1:T(4,128)}, u32[]{:S(2)}) copy-start(f32[4,6,11]{2,0,1:T(4,128)} %param.16) | copy-start | bytes 3172
  18.4 7.2 %copy-start.32 = (bf16[384]{0:T(512)(128)(2,1)S(1)}, bf16[384]{0:T(512)(128)(2,1)}, u32[]{:S(2)}) copy-start(bf16[384]{0:T(512)(128)(2,1)} %param.18) | copy-start | bytes 2308
  25.7 4.7 copy-start.26
  40.8 2.8 copy-start.17
  43.7 7.9 %copy-start.5 = (s32[1040,1]{1,0:T(8,128)S(1)}, s32[1040,1]{1,0:T(8,128)}, u32[]{:S(2)}) copy-start(s32[1040,1]{1,0:T(8,128)} %broadcast_in_dim.13.start_ref) | copy-start | bytes 12484
  51.6 40.8 %copy-start = (bf16[1024,1536]{1,0:T(8,128)(2,1)}, bf16[1024,1536]{1,0:T(8,128)(2,1)S(1)}, u32[]{:S(2)}) copy-start(bf16[1024,1536]{1,0:T(8,128)(2,1)S(1)} %convolution_convert_fusion.q_ref.k_ref.v_ref) | copy-start | bytes 9437188
  92.4 1.3 copy-start.7
  93.7 1.0 copy-start.9
  94.7 1.1 copy-start.1
  95.8 1.4 copy-start.2
  97.2 1.2 copy-start.10
  141.6 6.9 %copy-start.4 = (f32[1024,384]{1,0:T(8,128)}, f32[1024,384]{1,0:T(8,128)S(1)}, u32[]{:S(2)}) copy-start(f32[1024,384]{1,0:T(8,128)S(1)} %get-tuple-element.46.hidden_local_ref.hidden_ref) | copy-start | bytes 4718596
  141.6 6.9 %copy-start.15 = (bf16[1024,1536]{1,0:T(8,128)(2,1)S(1)}, bf16[1024,1536]{1,0:T(8,128)(2,1)}, u32[]{:S(2)}) copy-start(bf16[1024,1536]{1,0:T(8,128)(2,1)} %all-gather.5.cloned.1.call-done.cot_ref) | copy-start | bytes 9437188
  141.6 6.9 %copy-start.19 = (bf16[1024,1536]{1,0:T(8,128)(2,1)S(1)}, bf16[1024,1536]{1,0:T(8,128)(2,1)}, u32[]{:S(2)}) copy-start(bf16[1024,1536]{1,0:T(8,128)(2,1)} %w_down_ref.1) | copy-start | bytes 9437188
  141.6 10.3 %slice-start = ((s8[6291456]{0:T(1024)(128)(4,1)}), s8[4194304]{0:T(1024)(128)(4,1)S(1)}, s32[]{:S(2)}) async-start(s8[6291456]{0:T(1024)(128)(4,1)} %bitcast.70), calls=%async_computation.3 | async-start | bytes 8388608
  148.5 3.5 slice-start.1
  148.5 3.5 copy-start.33
  158.2 5.0 copy-start.22
  158.2 5.0 copy-start.23
  168.1 0.7 copy-start.29
  168.1 1.2 copy-start.30
  171.1 52.8 %copy-start.3 = (bf16[4,128,1536]{2,1,0:T(8,128)(2,1)S(1)}, bf16[4,128,1536]{2,1,0:T(8,128)(2,1)}, u32[]{:S(2)}) copy-start(bf16[4,128,1536]{2,1,0:T(8,128)(2,1)} %pad.41) | copy-start | bytes 4718596
  223.9 3.9 copy-start.6
  223.9 3.9 copy-start.8
  227.9 70.2 %copy-start.11 = (bf16[1024,512]{1,0:T(8,128)(2,1)S(1)}, bf16[1024,512]{1,0:T(8,128)(2,1)}, u32[]{:S(2)}) copy-start(bf16[1024,512]{1,0:T(8,128)(2,1)} %copy-done.9) | copy-start | bytes 3145732
  296.9 0.6 copy-start.13
  298.0 5.1 copy-start.31
  298.0 5.7 %copy-start.20 = (bf16[1024,1152]{1,0:T(8,128)(2,1)S(1)}, bf16[1024,1152]{1,0:T(8,128)(2,1)}, u32[]{:S(2)}) copy-start(bf16[1024,1152]{1,0:T(8,128)(2,1)} %get-tuple-element.48.grad_ref) | copy-start | bytes 7077892
  303.8 5.0 copy-start.18
  311.9 3.1 copy-start.21
  311.9 3.4 copy-start.34
  543.1 5.6 copy-start.25
  550.5 5.6 copy-start.14
  550.5 5.6 copy-start.16
  556.1 5.6 copy-start.27
  556.1 6.5 %copy-start.24 = (f32[1024,384]{1,0:T(8,128)S(1)}, f32[1024,384]{1,0:T(8,128)}, u32[]{:S(2)}) copy-start(f32[1024,384]{1,0:T(8,128)} %get-tuple-element.121) | copy-start | bytes 4718596
Sparse Core Ops, SparseCore 0:
  9.6 31.2 all-gather.2
  42.4 28.4 all-gather.4
  168.3 245.8 all-reduce.11
